TPU v7x, 32 devices: a whole 2x2x4 slice. The times are simulated.
32 devices in a mesh: row: 8 (over z, x), col: 4 (over y, core).
Axes of the slice: x: 2, y: 2, z: 4, core: 2. Of those that a mesh axis runs over, the one named last changes fastest.
Arguments:
- inputs: bfloat16 [4, 2048, 768], P(None, ('row', 'col')), may hold values from -6 to 6
- cotangent: bfloat16 [4, 2048, 768], P(None, ('row', 'col')), may hold values from -16 to 16
- projector: bfloat16 [768, 2304], P('row', 'col'), may hold values from -0.21875 to 0.21875
- projector_bias: bfloat16 [2304], P('col'), may hold values from -2 to 2
- combiner: bfloat16 [768, 768], P('row', 'col'), may hold values from -6 to 6
- combiner_bias: float32 [768], replicated, may hold values from -2 to 2
- attend_gain: float32 [768], replicated, may hold values from 0.5 to 1.5
- attend_shift: float32 [768], replicated, may hold values from -2 to 2
- expander: bfloat16 [768, 3072], P('row', 'col'), may hold values from -0.21875 to 0.21875
- expander_bias: bfloat16 [3072], P('col'), may hold values from -2 to 2
- reducer: bfloat16 [3072, 768], P('col', 'row'), may hold values from -0.109375 to 0.109375
- reducer_bias: float32 [768], replicated, may hold values from -2 to 2
- final_gain: float32 [768], replicated, may hold values from 0.5 to 1.5
- final_shift: float32 [768], replicated, may hold values from -2 to 2
- projection: float32 [256, 64], replicated, may hold values from -4 to 4
- lengths: int32 [4], replicated, may hold values from 512 to 2048, as said below
Outputs:
- layer_output: bfloat16 [4, 2048, 768], P(None, ('row', 'col'))
- input_gradient: float32 [4, 2048, 768], P(None, ('row', 'col'))
- grad_projector: float32 [768, 2304], P('row', 'col')
- grad_projector_bias: float32 [2304], P('col')
- grad_combiner: float32 [768, 768], P('row', 'col')
- grad_combiner_bias: float32 [768], replicated
- grad_attend_gain: float32 [768], replicated
- grad_attend_shift: float32 [768], replicated
- grad_expander: float32 [768, 3072], P('row', 'col')
- grad_expander_bias: float32 [3072], P('col')
- grad_reducer: float32 [3072, 768], P('col', 'row')
- grad_reducer_bias: float32 [768], replicated
- grad_final_gain: float32 [768], replicated
- grad_final_shift: float32 [768], replicated
Inputs may be any that keep to these rules, and one draw needn't show every extreme that they name: `lengths`: slots at or past a sequence's length are padding. One sequence has 2048 valid slots and one has 512.
All inputs are finite; a program needn't handle non-finite values.
Results may differ from a plain program's by a relative error of at most 0.018.
Values may be sent and summed in bfloat16 or wider, within the bound.
No kernel may reach another device: no remote copies, remote signals or barrier semaphores. Data moves between devices by JAX's collectives and lax.ppermute only.
A program may use at most 192 MiB of HBM per device.

v0:
```python
import jax
import jax.numpy as jnp
from jax import lax
from jax.sharding import PartitionSpec as P

layer_eps = 1e-06
largest_logit = lax.Precision.HIGHEST


def layer_norm(values, gain_vector, shift_vector):
    midpoint_shift = values - jnp.mean(values, axis=-1, keepdims=True)
    spread = jnp.mean(midpoint_shift * midpoint_shift, axis=-1, keepdims=True)
    return midpoint_shift * lax.rsqrt(spread + layer_eps) * gain_vector + shift_vector


def feature_map(vectors, omegas):
    scaled = vectors * vectors.shape[-1] ** (-0.25)
    angles = jnp.einsum("thd,md->thm", scaled, omegas, precision=largest_logit)
    energy = 0.5 * jnp.sum(scaled * scaled, axis=-1, keepdims=True)
    return jnp.exp(angles - energy) * omegas.shape[0] ** (-0.5)


def key_summary(key_rows, value_matrix, keep_mask, omegas):
    key_random_features = feature_map(key_rows, omegas) * keep_mask[:, None, None]
    key_value_state = jnp.einsum(
        "oyu,oyb->yub", key_random_features, value_matrix, precision=largest_logit
    )
    return (key_value_state, jnp.sum(key_random_features, axis=0))


def query_read(query_rows, key_value_state, norm_total, omegas):
    query_random_features = feature_map(query_rows, omegas)
    numerator_rows = jnp.einsum(
        "uow,owe->uoe", query_random_features, key_value_state, precision=largest_logit
    )
    denom = jnp.einsum("thm,hm->th", query_random_features, norm_total, precision=largest_logit)
    return numerator_rows / denom[:, :, None]


def exact_gelu(values):
    return jax.nn.gelu(values, approximate=False)


def contract_rows(left_mat, right_mat):
    return lax.dot_general(
        left_mat, right_mat, (((0,), (0,)), ((), ())), preferred_element_type=jnp.float32
    )


def contract_cols(left_mat, right_mat):
    return lax.dot_general(
        left_mat, right_mat, (((1,), (1,)), ((), ())), preferred_element_type=jnp.float32
    )


def fetch_weights(projector, combiner, expander, reducer, projector_bias, expander_bias):
    project_cols, expand_cols, reduce_cols = (projector, expander, reducer)
    pbias_cols, ebias_cols = (projector_bias, expander_bias)
    gathered = (
        lax.all_gather(project_cols, "row", axis=0, tiled=True),
        lax.all_gather(combiner, "row", axis=0, tiled=True),
        lax.all_gather(expand_cols, "row", axis=0, tiled=True),
        lax.all_gather(reduce_cols, "row", axis=1, tiled=True),
    )
    combine_full = lax.all_gather(gathered[1], "col", axis=1, tiled=True)
    return (
        gathered[0],
        combine_full,
        gathered[2],
        gathered[3],
        pbias_cols.astype(jnp.float32),
        ebias_cols.astype(jnp.float32),
    )


def reduce_grads(project_sum, combine_sum, expand_sum, reduce_sum, pbias_sum, ebias_sum):
    combine_cols = lax.psum_scatter(
        combine_sum.astype(jnp.bfloat16), "col", scatter_dimension=1, tiled=True
    )
    row_total = lax.axis_size("row")
    reduced = (
        lax.psum_scatter(
            project_sum.astype(jnp.bfloat16), "row", scatter_dimension=0, tiled=True
        ).astype(jnp.float32),
        lax.psum_scatter(combine_cols, "row", scatter_dimension=0, tiled=True).astype(jnp.float32),
        lax.psum_scatter(
            expand_sum.astype(jnp.bfloat16), "row", scatter_dimension=0, tiled=True
        ).astype(jnp.float32),
        lax.psum_scatter(
            reduce_sum.astype(jnp.bfloat16), "row", scatter_dimension=1, tiled=True
        ).astype(jnp.float32),
        lax.psum_scatter(
            jnp.tile(pbias_sum, row_total).astype(jnp.bfloat16),
            "row",
            scatter_dimension=0,
            tiled=True,
        ).astype(jnp.float32),
        lax.psum_scatter(
            jnp.tile(ebias_sum, row_total).astype(jnp.bfloat16),
            "row",
            scatter_dimension=0,
            tiled=True,
        ).astype(jnp.float32),
    )
    return reduced


def on_device(
    inputs,
    cotangent,
    projector,
    projector_bias,
    combiner,
    combiner_bias,
    attend_gain,
    attend_shift,
    expander,
    expander_bias,
    reducer,
    reducer_bias,
    final_gain,
    final_shift,
    projection,
    lengths,
):
    row_total = lax.axis_size("row")
    col_total = lax.axis_size("col")
    micro_count = inputs.shape[0]
    token_count = inputs.shape[1]
    model_width = inputs.shape[2]
    head_size = projection.shape[1]
    head_count = model_width // head_size
    seq_slots = lengths.shape[0] // micro_count
    seq_length = token_count * row_total * col_total // seq_slots
    first_slot = (lax.axis_index("row") * col_total + lax.axis_index("col")) * token_count
    seq_place = first_slot // seq_length
    positions = first_slot % seq_length + jnp.arange(token_count, dtype=jnp.int32)
    slot_hot = (jnp.arange(seq_slots, dtype=jnp.int32) == seq_place).astype(jnp.float32)
    slot_four = slot_hot[:, None, None, None]
    slot_three = slot_hot[:, None, None]

    def micro_step(micro_index, weights):
        project_full, combine_full, expand_full, reduce_full, pbias_f, ebias_f = weights
        token_rows = inputs[micro_index]
        token_group = lax.all_gather(token_rows, "col", axis=0, tiled=True)
        mixed_local = (
            jnp.dot(token_group, project_full, preferred_element_type=jnp.float32) + pbias_f
        ).astype(jnp.bfloat16)
        mixed = lax.all_to_all(mixed_local, "col", split_axis=0, concat_axis=1, tiled=True)
        mixed_f = mixed.astype(jnp.float32)
        query_rows = mixed_f[:, :model_width].reshape(token_count, head_count, head_size)
        key_rows = mixed_f[:, model_width : 2 * model_width].reshape(
            token_count, head_count, head_size
        )
        value_matrix = mixed_f[:, 2 * model_width :].reshape(token_count, head_count, head_size)
        seq_bound = lengths[micro_index * seq_slots + seq_place]
        keep_mask = (positions < seq_bound).astype(jnp.float32)
        key_value_state, norm_total = key_summary(key_rows, value_matrix, keep_mask, projection)
        state_sums = lax.psum(
            (slot_four * key_value_state[None], slot_three * norm_total[None]), ("row", "col")
        )
        state_all = jnp.sum(slot_four * state_sums[0], axis=0)
        total_all = jnp.sum(slot_three * state_sums[1], axis=0)
        attended = (
            query_read(query_rows, state_all, total_all, projection)
            .reshape(token_count, model_width)
            .astype(jnp.bfloat16)
        )
        branch = jnp.dot(attended, combine_full, preferred_element_type=jnp.float32) + combiner_bias
        resid_attend = token_rows.astype(jnp.float32) + branch
        normed = layer_norm(resid_attend, attend_gain, attend_shift).astype(jnp.bfloat16)
        normed_group = lax.all_gather(normed, "col", axis=0, tiled=True)
        pre_act = jnp.dot(normed_group, expand_full, preferred_element_type=jnp.float32) + ebias_f
        hidden = exact_gelu(pre_act).astype(jnp.bfloat16)
        shrunk = (
            lax.psum_scatter(
                jnp.dot(hidden, reduce_full, preferred_element_type=jnp.float32).astype(
                    jnp.bfloat16
                ),
                "col",
                scatter_dimension=0,
                tiled=True,
            ).astype(jnp.float32)
            + reducer_bias
        )
        resid_final = normed.astype(jnp.float32) + shrunk
        layer_out, final_pull = jax.vjp(layer_norm, resid_final, final_gain, final_shift)
        grad_final, grad_fgain, grad_fshift = final_pull(cotangent[micro_index].astype(jnp.float32))
        shrink_grad = grad_final.astype(jnp.bfloat16)
        shrink_group = lax.all_gather(shrink_grad, "col", axis=0, tiled=True)
        hidden_grad = contract_cols(shrink_group, reduce_full)
        reduce_part = contract_rows(hidden, shrink_group)
        gelu_pull = jax.vjp(exact_gelu, pre_act)[1]
        pre_grad = gelu_pull(hidden_grad)[0].astype(jnp.bfloat16)
        expand_part = contract_rows(normed_group, pre_grad)
        ebias_part = jnp.sum(pre_grad.astype(jnp.float32), axis=0)
        normed_grad = grad_final + lax.psum_scatter(
            contract_cols(pre_grad, expand_full).astype(jnp.bfloat16),
            "col",
            scatter_dimension=0,
            tiled=True,
        ).astype(jnp.float32)
        attend_pull = jax.vjp(layer_norm, resid_attend, attend_gain, attend_shift)[1]
        resid_grad, grad_again, grad_ashift = attend_pull(normed_grad)
        branch_grad = resid_grad.astype(jnp.bfloat16)
        combine_part = contract_rows(attended, branch_grad)
        attended_grad = contract_cols(branch_grad, combine_full)
        read_pull = jax.vjp(
            lambda query_in, state_in, total_in: query_read(
                query_in, state_in, total_in, projection
            ),
            query_rows,
            state_all,
            total_all,
        )[1]
        query_grad, state_grad, total_grad = read_pull(
            attended_grad.reshape(token_count, head_count, head_size)
        )
        small_terms = jnp.stack(
            [
                grad_fgain,
                grad_fshift,
                grad_again,
                grad_ashift,
                jnp.sum(branch_grad.astype(jnp.float32), axis=0),
                jnp.sum(shrink_grad.astype(jnp.float32), axis=0),
            ]
        )
        summed = lax.psum(
            (slot_four * state_grad[None], slot_three * total_grad[None], small_terms),
            ("row", "col"),
        )
        state_back = jnp.sum(slot_four * summed[0], axis=0)
        total_back = jnp.sum(slot_three * summed[1], axis=0)
        summary_pull = jax.vjp(
            lambda key_in, value_in: key_summary(key_in, value_in, keep_mask, projection),
            key_rows,
            value_matrix,
        )[1]
        key_grad, value_grad = summary_pull((state_back, total_back))
        mixed_grad = jnp.concatenate(
            [
                query_grad.reshape(token_count, model_width),
                key_grad.reshape(token_count, model_width),
                value_grad.reshape(token_count, model_width),
            ],
            axis=1,
        ).astype(jnp.bfloat16)
        mixed_group = lax.all_to_all(mixed_grad, "col", split_axis=1, concat_axis=0, tiled=True)
        project_part = contract_rows(token_group, mixed_group)
        pbias_part = jnp.sum(mixed_group.astype(jnp.float32), axis=0)
        input_grad = resid_grad + lax.psum_scatter(
            contract_cols(mixed_group, project_full).astype(jnp.bfloat16),
            "col",
            scatter_dimension=0,
            tiled=True,
        ).astype(jnp.float32)
        parts = (project_part, combine_part, expand_part, reduce_part, pbias_part, ebias_part)
        return (layer_out.astype(jnp.bfloat16), input_grad, parts, summed[2])

    layer_outs = []
    input_grads = []
    small_acc = jnp.zeros((6, model_width), jnp.float32)
    shard_acc = (
        jnp.zeros(projector.shape, jnp.float32),
        jnp.zeros(combiner.shape, jnp.float32),
        jnp.zeros(expander.shape, jnp.float32),
        jnp.zeros(reducer.shape, jnp.float32),
        jnp.zeros(projector_bias.shape, jnp.float32),
        jnp.zeros(expander_bias.shape, jnp.float32),
    )
    for micro_index in range(micro_count):
        weights = fetch_weights(
            projector, combiner, expander, reducer, projector_bias, expander_bias
        )
        layer_out, input_grad, parts, small_sums = micro_step(micro_index, weights)
        layer_outs.append(layer_out)
        input_grads.append(input_grad)
        small_acc = small_acc + small_sums
        reduced = reduce_grads(*parts)
        shard_acc = tuple((running + update for running, update in zip(shard_acc, reduced)))
    return (
        jnp.stack(layer_outs),
        jnp.stack(input_grads),
        shard_acc[0],
        shard_acc[4],
        shard_acc[1],
        small_acc[4],
        small_acc[2],
        small_acc[3],
        shard_acc[2],
        shard_acc[5],
        shard_acc[3],
        small_acc[5],
        small_acc[0],
        small_acc[1],
    )


def solution(mesh):
    placed = (
        P(None, ("row", "col"), None),
        P(None, ("row", "col"), None),
        P("row", "col"),
        P("col"),
        P("row", "col"),
        P(),
        P(),
        P(),
        P("row", "col"),
        P("col"),
        P("col", "row"),
        P(),
        P(),
        P(),
        P(),
        P(),
    )
    return jax.shard_map(
        on_device,
        mesh=mesh,
        in_specs=placed,
        out_specs=(
            P(None, ("row", "col"), None),
            P(None, ("row", "col"), None),
            P("row", "col"),
            P("col"),
            P("row", "col"),
            P(),
            P(),
            P(),
            P("row", "col"),
            P("col"),
            P("col", "row"),
            P(),
            P(),
            P(),
        ),
        check_vma=False,
    )
```

profile of v0, /device:TPU:0, one launch (start us, length us, event | category | flops | bytes accessed | tf_op | source)
XLA Modules:
  0.0 1893.2 jit_solution(9473335730361034440)
XLA Ops:
  8.1 34.7 %all_gather.67 = bf16[768,576]{1,0:T(8,128)(2,1)S(1)} all-gather(bf16[96,576]{1,0:T(8,128)(2,1)} %param.18), channel_id=1, replica_groups=mesh['row'=8,'col'=4] {'row'}, dimensions={0}, use_global_device_ids=true | all-gather | bytes 995328 | tf_op jit(solution)/shard_map/all_gather | solution.py:60
  123.7 31.8 %all_gather.68 = bf16[768,192]{1,0:T(8,128)(2,1)S(1)} all-gather(bf16[96,192]{1,0:T(8,128)(2,1)S(1)} %copy-done.168), channel_id=1, replica_groups=mesh['row'=8,'col'=4] {'row'}, dimensions={0}, use_global_device_ids=true | all-gather | bytes 331776 | tf_op jit(solution)/shard_map/all_gather | solution.py:61
  161.3 39.9 %all-reduce.9 = (f32[1,12,256]{2,1,0:T(8,128)S(1)}, f32[1,12,256]{2,1,0:T(8,128)S(1)}, f32[1,12,256]{2,1,0:T(8,128)S(1)}, f32[1,12,256]{2,1,0:T(8,128)S(1)}) all-reduce(f32[1,12,256]{2,1,0:T(8,128)S(1)} %multiply_bitcast_fusion.7, f32[1,12,256]{2,1,0:T(8,128)S(1)} %multiply_bitcast_fusion.5, ...), channel_id=1, replica_groups=mesh['row'=8,'col'=4] {'row','col'}, use_global_device_ids=true, to_apply=%region_4.5 | all-reduce | flops 12288 | bytes 98304 | tf_op jit(solution)/shard_map/psum | solution.py:159
  212.7 59.8 %all-reduce.22.cloned.1.call-done = (f32[1,12,256,64]{2,3,1,0:T(8,128)}, f32[1,12,256,64]{2,3,1,0:T(8,128)}, f32[1,12,256,64]{2,3,1,0:T(8,128)}, f32[1,12,256,64]{2,3,1,0:T(8,128)}) async-done(((f32[1,12,256,64]{2,3,1,0:T(8,128)}, f32[1,12,256,64]{2,3,1,0:T(8,128)}, f32[1,12,256,64]{2,3,1,0:T(8,128)}, f32[1,12,256,64]{2,3,1,0:T(8,128)}), (f32[1,12,256,64]{2,3,1,0:T(8,128)}, f32[1,12,256,64]{2,3,1,0:T(8,128)}, ...) | async-done | bytes 3145744 | tf_op jit(solution)/shard_map/psum | solution.py:159
  389.3 23.3 %reduce-scatter.55.cloned.1.call-done = bf16[64,768]{1,0:T(8,128)(2,1)} async-done(((bf16[256,768]{1,0:T(8,128)(2,1)}), bf16[64,768]{1,0:T(8,128)(2,1)}) %reduce-scatter.55.cloned.1.call-update) | async-done | bytes 98320 | tf_op jit(solution)/shard_map/reduce_scatter | solution.py:176
  591.5 79.0 %all-reduce.18.cloned.1.call-done = (f32[1,12,256]{2,1,0:T(8,128)}, f32[1,12,256]{2,1,0:T(8,128)}, f32[1,12,256]{2,1,0:T(8,128)}, f32[1,12,256]{2,1,0:T(8,128)}, f32[6,768]{1,0:T(8,128)}) async-done(((f32[1,12,256]{2,1,0:T(8,128)}, f32[1,12,256]{2,1,0:T(8,128)}, f32[1,12,256]{2,1,0:T(8,128)}, f32[1,12,256]{2,1,0:T(8,128)}, f32[6,768]{1,0:T(8,128)}), (f32[1,12,256]{2,1,0:T(8,128)}, f32[1,12,256]{2,1,0:T(8,128)}, ...) | async-done | bytes 67600 | tf_op jit(solution)/shard_map/psum | solution.py:229
  673.3 151.3 %all-reduce.20.cloned.1.call-done = (f32[1,12,256,64]{2,3,1,0:T(8,128)}, f32[1,12,256,64]{2,3,1,0:T(8,128)}, f32[1,12,256,64]{2,3,1,0:T(8,128)}, f32[1,12,256,64]{2,3,1,0:T(8,128)}) async-done(((f32[1,12,256,64]{2,3,1,0:T(8,128)}, f32[1,12,256,64]{2,3,1,0:T(8,128)}, f32[1,12,256,64]{2,3,1,0:T(8,128)}, f32[1,12,256,64]{2,3,1,0:T(8,128)}), (f32[1,12,256,64]{2,3,1,0:T(8,128)}, f32[1,12,256,64]{2,3,1,0:T(8,128)}, ...) | async-done | bytes 3145744 | tf_op jit(solution)/shard_map/psum | solution.py:229
  899.4 28.9 %reduce-scatter.81.cloned.1.call-done = bf16[96,768]{1,0:T(8,128)(2,1)} async-done(((bf16[768,768]{1,0:T(8,128)(2,1)}), bf16[96,768]{1,0:T(8,128)(2,1)}) %reduce-scatter.81.cloned.1.call-update) | async-done | bytes 147472 | tf_op jit(solution)/shard_map/reduce_scatter | solution.py:86
  932.1 63.3 %reduce-scatter.95.cloned.1.call-done = bf16[768,96]{0,1:T(8,128)(2,1)} async-done(((bf16[768,768]{0,1:T(8,128)(2,1)}), bf16[768,96]{0,1:T(8,128)(2,1)}) %reduce-scatter.95.cloned.1.call-update) | async-done | bytes 147472 | tf_op jit(solution)/shard_map/reduce_scatter | solution.py:89
  995.4 67.0 %reduce-scatter.93.cloned.1.call-done = bf16[768,96]{0,1:T(8,128)(2,1)} async-done(((bf16[768,768]{0,1:T(8,128)(2,1)}), bf16[768,96]{0,1:T(8,128)(2,1)}) %reduce-scatter.93.cloned.1.call-update) | async-done | bytes 147472 | tf_op jit(solution)/shard_map/reduce_scatter | solution.py:89
  1062.4 67.0 %reduce-scatter.91.cloned.1.call-done = bf16[768,96]{0,1:T(8,128)(2,1)} async-done(((bf16[768,768]{0,1:T(8,128)(2,1)}), bf16[768,96]{0,1:T(8,128)(2,1)}) %reduce-scatter.91.cloned.1.call-update) | async-done | bytes 147472 | tf_op jit(solution)/shard_map/reduce_scatter | solution.py:89
  1129.4 66.9 %reduce-scatter.89.cloned.1.call-done = bf16[768,96]{0,1:T(8,128)(2,1)} async-done(((bf16[768,768]{0,1:T(8,128)(2,1)}), bf16[768,96]{0,1:T(8,128)(2,1)}) %reduce-scatter.89.cloned.1.call-update) | async-done | bytes 147472 | tf_op jit(solution)/shard_map/reduce_scatter | solution.py:89
  1198.2 72.9 %all-reduce.24.cloned.1.call-done = (bf16[4608]{0:T(1024)(128)(2,1)}, bf16[4608]{0:T(1024)(128)(2,1)}, bf16[4608]{0:T(1024)(128)(2,1)}, bf16[4608]{0:T(1024)(128...) async-done(((bf16[4608]{0:T(1024)(128)(2,1)}, bf16[4608]{0:T(1024)(128)(2,1)}, ...) | async-done | bytes 86032
  1295.1 22.3 %reduce-scatter.67.cloned.1.call-done = bf16[64,768]{1,0:T(8,128)(2,1)} async-done(((bf16[256,768]{1,0:T(8,128)(2,1)}), bf16[64,768]{1,0:T(8,128)(2,1)}) %reduce-scatter.67.cloned.1.call-update) | async-done | bytes 98320 | tf_op jit(solution)/shard_map/reduce_scatter | solution.py:252
  1318.4 22.3 %reduce-scatter.63.cloned.1.call-done = bf16[64,768]{1,0:T(8,128)(2,1)} async-done(((bf16[256,768]{1,0:T(8,128)(2,1)}), bf16[64,768]{1,0:T(8,128)(2,1)}) %reduce-scatter.63.cloned.1.call-update) | async-done | bytes 98320 | tf_op jit(solution)/shard_map/reduce_scatter | solution.py:252
  1341.7 22.1 %reduce-scatter.59.cloned.1.call-done = bf16[64,768]{1,0:T(8,128)(2,1)} async-done(((bf16[256,768]{1,0:T(8,128)(2,1)}), bf16[64,768]{1,0:T(8,128)(2,1)}) %reduce-scatter.59.cloned.1.call-update) | async-done | bytes 98320 | tf_op jit(solution)/shard_map/reduce_scatter | solution.py:252
  1365.8 62.7 %reduce-scatter.111.cloned.1.call-done = bf16[96,192]{1,0:T(8,128)(2,1)} async-done(((bf16[768,192]{1,0:T(8,128)(2,1)}), bf16[96,192]{1,0:T(8,128)(2,1)}) %reduce-scatter.111.cloned.1.call-update) | async-done | bytes 36880
  1429.4 62.9 %reduce-scatter.109.cloned.1.call-done = bf16[96,192]{1,0:T(8,128)(2,1)} async-done(((bf16[768,192]{1,0:T(8,128)(2,1)}), bf16[96,192]{1,0:T(8,128)(2,1)}) %reduce-scatter.109.cloned.1.call-update) | async-done | bytes 36880
  1493.2 62.7 %reduce-scatter.107.cloned.1.call-done = bf16[96,192]{1,0:T(8,128)(2,1)} async-done(((bf16[768,192]{1,0:T(8,128)(2,1)}), bf16[96,192]{1,0:T(8,128)(2,1)}) %reduce-scatter.107.cloned.1.call-update) | async-done | bytes 36880
  1556.9 62.7 %reduce-scatter.105.cloned.1.call-done = bf16[96,192]{1,0:T(8,128)(2,1)} async-done(((bf16[768,192]{1,0:T(8,128)(2,1)}), bf16[96,192]{1,0:T(8,128)(2,1)}) %reduce-scatter.105.cloned.1.call-update) | async-done | bytes 36880
  1621.3 64.1 %reduce-scatter.103.cloned.1.call-done = bf16[96,576]{1,0:T(8,128)(2,1)} async-done(((bf16[768,576]{1,0:T(8,128)(2,1)}), bf16[96,576]{1,0:T(8,128)(2,1)}) %reduce-scatter.103.cloned.1.call-update) | async-done | bytes 110608
  1686.4 65.1 %reduce-scatter.101.cloned.1.call-done = bf16[96,576]{1,0:T(8,128)(2,1)} async-done(((bf16[768,576]{1,0:T(8,128)(2,1)}), bf16[96,576]{1,0:T(8,128)(2,1)}) %reduce-scatter.101.cloned.1.call-update) | async-done | bytes 110608
  1752.6 64.7 %reduce-scatter.99.cloned.1.call-done = bf16[96,576]{1,0:T(8,128)(2,1)} async-done(((bf16[768,576]{1,0:T(8,128)(2,1)}), bf16[96,576]{1,0:T(8,128)(2,1)}) %reduce-scatter.99.cloned.1.call-update) | async-done | bytes 110608
  1818.2 65.2 %reduce-scatter.97.cloned.1.call-done = bf16[96,576]{1,0:T(8,128)(2,1)} async-done(((bf16[768,576]{1,0:T(8,128)(2,1)}), bf16[96,576]{1,0:T(8,128)(2,1)}) %reduce-scatter.97.cloned.1.call-update) | async-done | bytes 110608
  (1054 shorter events, 508.7 us)
Async XLA Ops:
  540.6 341.8 %reduce-scatter.79.cloned.1.call-start = ((), (), s32[]{:S(2)}) async-start(), calls=%async_computation.58 | async-start | bytes 1474560 | tf_op jit(solution)/shard_map/reduce_scatter | solution.py:77
  544.7 341.7 %reduce-scatter.75.cloned.1.call-start = ((), (), s32[]{:S(2)}) async-start(), calls=%async_computation.56 | async-start | bytes 1474560 | tf_op jit(solution)/shard_map/reduce_scatter | solution.py:77
  546.4 342.1 %reduce-scatter.73.cloned.1.call-start = ((), (), s32[]{:S(2)}) async-start(), calls=%async_computation.55 | async-start | bytes 1474560 | tf_op jit(solution)/shard_map/reduce_scatter | solution.py:77
  548.0 351.4 %reduce-scatter.87.cloned.1.call-start = ((), (), s32[]{:S(2)}) async-start(), calls=%async_computation.62 | async-start | bytes 1327104 | tf_op jit(solution)/shard_map/reduce_scatter | solution.py:86
  550.7 348.7 %reduce-scatter.85.cloned.1.call-start = ((), (), s32[]{:S(2)}) async-start(), calls=%async_computation.61 | async-start | bytes 1327104 | tf_op jit(solution)/shard_map/reduce_scatter | solution.py:86
  553.4 346.0 %reduce-scatter.83.cloned.1.call-start = ((), (), s32[]{:S(2)}) async-start(), calls=%async_computation.60 | async-start | bytes 1327104 | tf_op jit(solution)/shard_map/reduce_scatter | solution.py:86
  556.1 372.2 %reduce-scatter.81.cloned.1.call-start = ((), (), s32[]{:S(2)}) async-start(), calls=%async_computation.59 | async-start | bytes 1327104 | tf_op jit(solution)/shard_map/reduce_scatter | solution.py:86
  558.9 436.6 %reduce-scatter.95.cloned.1.call-start = ((), (), s32[]{:S(2)}) async-start(), calls=%async_computation.66 | async-start | bytes 1327104 | tf_op jit(solution)/shard_map/reduce_scatter | solution.py:89
  561.5 500.9 %reduce-scatter.93.cloned.1.call-start = ((), (), s32[]{:S(2)}) async-start(), calls=%async_computation.65 | async-start | bytes 1327104 | tf_op jit(solution)/shard_map/reduce_scatter | solution.py:89
  564.2 565.1 %reduce-scatter.91.cloned.1.call-start = ((), (), s32[]{:S(2)}) async-start(), calls=%async_computation.64 | async-start | bytes 1327104 | tf_op jit(solution)/shard_map/reduce_scatter | solution.py:89
  566.9 629.5 %reduce-scatter.89.cloned.1.call-start = ((), (), s32[]{:S(2)}) async-start(), calls=%async_computation.63 | async-start | bytes 1327104 | tf_op jit(solution)/shard_map/reduce_scatter | solution.py:89
  869.4 401.8 %all-reduce.24.cloned.1.call-start = ((), (), s32[]{:S(2)}) async-start(), calls=%async_computation.78 | async-start | bytes 180224
  876.9 417.3 %reduce-scatter.71.cloned.1.call-start = ((), (), s32[]{:S(2)}) async-start(), calls=%async_computation.54 | async-start | bytes 491520 | tf_op jit(solution)/shard_map/reduce_scatter | solution.py:252
  878.2 439.2 %reduce-scatter.67.cloned.1.call-start = ((), (), s32[]{:S(2)}) async-start(), calls=%async_computation.52 | async-start | bytes 491520 | tf_op jit(solution)/shard_map/reduce_scatter | solution.py:252
  879.6 461.1 %reduce-scatter.63.cloned.1.call-start = ((), (), s32[]{:S(2)}) async-start(), calls=%async_computation.50 | async-start | bytes 491520 | tf_op jit(solution)/shard_map/reduce_scatter | solution.py:252
  880.9 482.9 %reduce-scatter.59.cloned.1.call-start = ((), (), s32[]{:S(2)}) async-start(), calls=%async_computation.48 | async-start | bytes 491520 | tf_op jit(solution)/shard_map/reduce_scatter | solution.py:252
  882.3 546.2 %reduce-scatter.111.cloned.1.call-start = ((), (), s32[]{:S(2)}) async-start(), calls=%async_computation.74 | async-start | bytes 442368
  884.3 608.0 %reduce-scatter.109.cloned.1.call-start = ((), (), s32[]{:S(2)}) async-start(), calls=%async_computation.73 | async-start | bytes 442368
  886.3 669.6 %reduce-scatter.107.cloned.1.call-start = ((), (), s32[]{:S(2)}) async-start(), calls=%async_computation.72 | async-start | bytes 442368
  888.3 731.2 %reduce-scatter.105.cloned.1.call-start = ((), (), s32[]{:S(2)}) async-start(), calls=%async_computation.71 | async-start | bytes 442368
  890.3 795.1 %reduce-scatter.103.cloned.1.call-start = ((), (), s32[]{:S(2)}) async-start(), calls=%async_computation.70 | async-start | bytes 1105920
  892.2 859.3 %reduce-scatter.101.cloned.1.call-start = ((), (), s32[]{:S(2)}) async-start(), calls=%async_computation.69 | async-start | bytes 1105920
  894.0 923.2 %reduce-scatter.99.cloned.1.call-start = ((), (), s32[]{:S(2)}) async-start(), calls=%async_computation.68 | async-start | bytes 1105920
  896.0 987.5 %reduce-scatter.97.cloned.1.call-start = ((), (), s32[]{:S(2)}) async-start(), calls=%async_computation.67 | async-start | bytes 1105920
  (298 other events, 8325.0 us)
Sparse Core Ops, SparseCore 0:
  123.0 149.3 all-reduce.21
  538.8 131.5 all-reduce.17
  678.0 146.5 all-reduce.19
Sparse Core Ops, SparseCore 1:
  176.2 41.4 all-gather.9
  219.8 42.9 all-gather.11
  429.6 21.1 reduce-scatter.64
  544.1 25.7 reduce-scatter.78
  572.3 25.7 reduce-scatter.76
  600.8 25.6 reduce-scatter.74
  629.1 25.9 reduce-scatter.72
  658.9 65.8 reduce-scatter.86
  728.5 63.5 reduce-scatter.84
  795.9 65.4 reduce-scatter.82
  865.0 63.2 reduce-scatter.80
  932.1 63.2 reduce-scatter.94
  999.1 63.3 reduce-scatter.92
  1066.0 63.3 reduce-scatter.90
  1133.0 63.2 reduce-scatter.88
  1201.2 69.9 all-reduce.23
  1367.0 61.4 reduce-scatter.110
  1431.8 60.5 reduce-scatter.108
  1495.5 60.4 reduce-scatter.106
  1559.1 60.4 reduce-scatter.104
  1623.0 62.4 reduce-scatter.102
  1689.0 62.5 reduce-scatter.100
  1754.7 62.4 reduce-scatter.98
  1820.9 62.4 reduce-scatter.96
  (12 shorter events, 243.4 us)
where the time goes:
time: 1900 us; the launch traced here: 1890 us
  waiting for transfers between devices  1380 us (73%)
  blocking collectives  192 us (10%)
  matrix products  133 us (7%)
  local copies, waits for them, and re-layouts  79.4 us (4%)
  other arithmetic  58.1 us (3%)
  starting transfers between devices  30.6 us (2%)
  between operations  21.7 us (1%)
    unnamed x48, waiting for transfers between devices  585 us
    reduce_scatter x4, waiting for transfers between devices, reduce_grads(): lax.psum_scatter(reduce_sum.astype(jnp.bfloat16), 'row', scatter_dimensio...  264 us
    psum x2, waiting for transfers between devices, micro_step(): lax.psum((slot_four * state_grad[None], slot_three * total_grad[None], sm...  230 us
    reduce_scatter x4, waiting for transfers between devices, micro_step(): lax.psum_scatter(contract_cols(mixed_group, project_full).astype(jnp.bflo...  87 us
    reduce_scatter x4, waiting for transfers between devices, micro_step(): lax.psum_scatter(jnp.dot(hidden, reduce_full, preferred_element_type=jnp....  63.6 us
    psum x1, waiting for transfers between devices, micro_step(): lax.psum((slot_four * key_value_state[None], slot_three * norm_total[None...  59.8 us
    reduce_scatter x4, waiting for transfers between devices, micro_step(): lax.psum_scatter(contract_cols(pre_grad, expand_full).astype(jnp.bfloat16...  41.3 us
    psum x1, blocking collectives, micro_step(): lax.psum((slot_four * key_value_state[None], slot_three * norm_total[None...  39.9 us
  transfers between devices with their start and end apart: 47, of which 32 were waited for; matrix products, arithmetic and copies ran while one was open for 11% of the time, Pallas kernels for 0%

commit v1 on v0

v1 whole, which is shorter than its diff:
```python
import jax
import jax.numpy as jnp
from jax import lax
from jax.experimental import pallas as pl
from jax.experimental.pallas import tpu as pltpu
from jax.sharding import PartitionSpec as P

layer_eps = 1e-06
BF = jnp.bfloat16
F32 = jnp.float32
MIB = 1024 * 1024


def nt(left, right):
    return lax.dot_general(left, right, (((1,), (1,)), ((), ())), preferred_element_type=F32)


def tn(left, right):
    return lax.dot_general(left, right, (((0,), (0,)), ((), ())), preferred_element_type=F32)


def nn(left, right):
    return jnp.dot(left, right, preferred_element_type=F32)


def down(values):
    return jnp.sum(values, axis=0, keepdims=True)


def across(values):
    return jnp.sum(values, axis=1, keepdims=True)


def halves(shape):
    return lax.broadcasted_iota(jnp.int32, shape, 1) < shape[1] // 2


def beside(*parts):
    return jnp.concatenate(parts, axis=1)


def lanes_up(n):
    return -(-n // 128) * 128


def project_kernel(xh_ref, xf_ref, pa_ref, pb_ref, bias_ref, here_ref, away_ref):
    pa, pb, bias = pa_ref[0], pb_ref[0], bias_ref[0]
    extra = jnp.zeros((xh_ref.shape[0], bias.shape[1] - pa.shape[1] - pb.shape[1]), F32)
    for x_ref, out_ref in ((xh_ref, here_ref), (xf_ref, away_ref)):
        x = x_ref[...]
        out_ref[0] = (beside(nn(x, pa), nn(x, pb), extra) + bias).astype(BF)


def project_back_kernel(gh_ref, gf_ref, pa_ref, pb_ref, resid_ref, here_ref, away_ref, acc_ref):
    y = pl.program_id(0)
    cut = pa_ref.shape[2]

    @pl.when(y == 0)
    def _():
        here_ref[...] = resid_ref[...]
        acc_ref[...] = jnp.zeros_like(acc_ref)

    pa, pb = pa_ref[0], pb_ref[0]
    gh, gf = gh_ref[0], gf_ref[0]
    end = cut + pb.shape[1]
    here_ref[...] += nt(gh[:, :cut], pa) + nt(gh[:, cut:end], pb)
    acc_ref[...] += nt(gf[:, :cut], pa) + nt(gf[:, cut:end], pb)

    @pl.when(y == pl.num_programs(0) - 1)
    def _():
        away_ref[...] = acc_ref[...].astype(BF)


def pair_features(u, rhs, scale, weight):
    uf = u.astype(F32)
    squares = uf * uf * (0.5 * scale * scale)
    low = halves(squares.shape)
    first = across(jnp.where(low, squares, 0.0))
    second = across(jnp.where(low, 0.0, squares))
    angles = nn(beside(u, u), rhs)
    m = angles.shape[1] // 2
    return beside(jnp.exp(angles[:, :m] - first) * weight, jnp.exp(angles[:, m:] - second) * weight)


def pick(both):
    m = both.shape[0] // 2
    return jnp.where(halves((m, both.shape[1])), both[:m], both[m:])


def put_totals(msg_ref, tot_ref, base):
    msg_ref[base : base + tot_ref.shape[0]] = tot_ref[...].astype(BF)


def row_to_rows(tot_ref, start, row):
    n = tot_ref.shape[1]
    for k in range(row.shape[1] // n):
        tot_ref[start + k : start + k + 1] = row[:, k * n : (k + 1) * n]


def rows_to_row(msg_ref, start, count):
    rows = msg_ref[start : start + count].astype(F32)
    return beside(*[rows[k : k + 1] for k in range(count)])


def features_kernel(
    scale, weight, n_proj, idx_ref, here_ref, far_ref, rhs_ref, keep_ref, mixed_ref, fq_ref, fk_ref, msg_ref, tot_ref
):
    cols2 = here_ref.shape[0]
    lanes = keep_ref.shape[1]
    pairs, _, wide = fq_ref.shape
    feats = wide // 2

    def assemble(even, odd):
        mixed_ref[...] = beside(*[r[y][:, :n_proj] for y in range(cols2) for r in (even, odd)])

    pl.when(idx_ref[0] == 0)(lambda: assemble(here_ref, far_ref))
    pl.when(idx_ref[0] == 1)(lambda: assemble(far_ref, here_ref))
    rhs = rhs_ref[...]
    keep = keep_ref[:, :1]
    tot_ref[...] = jnp.zeros_like(tot_ref)
    per = wide // lanes

    def column(block):
        return mixed_ref[:, block * lanes : (block + 1) * lanes]

    for p in range(pairs):
        fk = (pair_features(column(pairs + p), rhs, scale, weight) * keep).astype(BF)
        fk_ref[p] = fk
        msg_ref[p * feats : (p + 1) * feats] = pick(tn(fk, column(2 * pairs + p))).astype(BF)
        row_to_rows(tot_ref, p * per, down(fk.astype(F32)))
        fq_ref[p] = pair_features(column(p), rhs, scale, weight).astype(BF)
    put_totals(msg_ref, tot_ref, pairs * feats)


def pair_sums(msg_ref, p, pairs, feats, per):
    return msg_ref[p * feats : (p + 1) * feats], rows_to_row(msg_ref, pairs * feats + p * per, per)


def read_pair(fq, st, total):
    feats, lanes = st.shape
    weighted = fq.astype(F32) * total
    low = halves((fq.shape[0], lanes))
    rd = 1.0 / jnp.where(low, across(weighted[:, :feats]), across(weighted[:, feats:]))
    return jnp.where(low, nn(fq[:, :feats], st), nn(fq[:, feats:], st)) * rd, rd


def pull_features(g, u, back, scale):
    both = nn(g, back)
    n = u.shape[1]
    return scale * (both[:, :n] - scale * both[:, n:] * u.astype(F32))


def query_back_pair(scale, da, a, rd, fq, st, total, u, back):
    feats = st.shape[0]
    dnum = (da * rd).astype(BF)
    prod = dnum.astype(F32) * a
    low = halves(prod.shape)
    dden0 = -across(jnp.where(low, prod, 0.0))
    dden1 = -across(jnp.where(low, 0.0, prod))
    none = jnp.zeros_like(dnum)
    fqf = fq.astype(F32)
    f0, f1 = fqf[:, :feats], fqf[:, feats:]
    g0 = (nt(jnp.where(low, dnum, none), st) + dden0 * total[:, :feats]) * f0
    g1 = (nt(jnp.where(low, none, dnum), st) + dden1 * total[:, feats:]) * f1
    dq = pull_features(beside(g0, g1).astype(BF), u, back, scale).astype(BF)
    return dq, pick(tn(fq, dnum)).astype(BF), beside(down(f0 * dden0), down(f1 * dden1))


def key_back_kernel(scale, n, idx_ref, fk_ref, msg_ref, mixed_ref, dq_ref, back_ref, here_ref, away_ref, all_ref):
    pairs, _, wide = fk_ref.shape
    feats, lanes = wide // 2, msg_ref.shape[1]
    per = wide // lanes
    back = back_ref[...]
    all_ref[:, : pairs * lanes] = dq_ref[...]
    for p in range(pairs):
        k_at = slice((pairs + p) * lanes, (pairs + p + 1) * lanes)
        v_at = slice((2 * pairs + p) * lanes, (2 * pairs + p + 1) * lanes)
        fk = fk_ref[p]
        sg = msg_ref[p * feats : (p + 1) * feats]
        tg = rows_to_row(msg_ref, pairs * feats + p * per, per)
        v = mixed_ref[:, v_at]
        low = halves(v.shape)
        zero = jnp.zeros_like(v)
        fkf = fk.astype(F32)
        g0 = (nt(jnp.where(low, v, zero), sg) + tg[:, :feats]) * fkf[:, :feats]
        g1 = (nt(jnp.where(low, zero, v), sg) + tg[:, feats:]) * fkf[:, feats:]
        all_ref[:, k_at] = pull_features(beside(g0, g1).astype(BF), mixed_ref[:, k_at], back, scale).astype(BF)
        all_ref[:, v_at] = jnp.where(low, nn(fk[:, :feats], sg), nn(fk[:, feats:], sg)).astype(BF)
    cols2, tokens, n_pad = here_ref.shape

    def share(even_ref, odd_ref):
        for y in range(cols2):
            for k, ref in ((0, even_ref), (1, odd_ref)):
                c = 2 * y + k
                block = all_ref[:, c * n : (c + 1) * n]
                ref[y] = beside(block, jnp.zeros((tokens, n_pad - n), BF)) if n_pad > n else block

    pl.when(idx_ref[0] == 0)(lambda: share(here_ref, away_ref))
    pl.when(idx_ref[0] == 1)(lambda: share(away_ref, here_ref))


def norm_parts(values):
    centred = values - jnp.mean(values, axis=-1, keepdims=True)
    r = lax.rsqrt(jnp.mean(centred * centred, axis=-1, keepdims=True) + layer_eps)
    return centred * r, r


def norm_pull(dy, vhat, r, gain):
    dg = dy * gain
    return r * (
        dg - jnp.mean(dg, axis=-1, keepdims=True) - vhat * jnp.mean(dg * vhat, axis=-1, keepdims=True)
    )


def middle_kernel(
    scale,
    idx_ref,
    fq_ref,
    msg_ref,
    q_ref,
    back_ref,
    x_ref,
    cot_ref,
    vec_ref,
    eb_ref,
    comb_own_ref,
    comb_far_ref,
    expd_own_ref,
    expd_far_ref,
    redu_own_ref,
    redu_far_ref,
    at_ref,
    out_ref,
    normed_ref,
    hid_here_ref,
    hid_away_ref,
    pre_here_ref,
    pre_away_ref,
    shrink_ref,
    bg_here_ref,
    bg_away_ref,
    resid_ref,
    sums_ref,
    ebg_here_ref,
    ebg_away_ref,
    dq_ref,
    msg_out_ref,
    acc_ref,
    vhat_ref,
    r_ref,
    gf_ref,
    slope_ref,
    a_ref,
    rd_ref,
    tot_ref,
):
    phase, c = pl.program_id(0), pl.program_id(1)
    cols = pl.num_programs(1)
    width = x_ref.shape[1]
    cols2 = hid_here_ref.shape[0]
    step = width // (2 * cols2)
    core = idx_ref[0]
    y, k = lax.div(c, 2), lax.rem(c, 2)
    pairs, _, wide = fq_ref.shape
    feats, lanes = wide // 2, msg_ref.shape[1]
    per = wide // lanes

    def comb(ref, b):
        rows = ref.shape[0] // cols2
        return ref[b * rows : (b + 1) * rows].reshape(width, -1)[:, :step]

    @pl.when((phase == 0) & (c == 0))
    def _():
        for p in range(pairs):
            here = slice(p * lanes, (p + 1) * lanes)
            a, rd = read_pair(fq_ref[p], *pair_sums(msg_ref, p, pairs, feats, per))
            a_ref[:, here] = a
            rd_ref[:, here] = rd
            at_ref[:, here] = a.astype(BF)
        at = at_ref[...]

        def attend(even_ref, odd_ref):
            acc_ref[...] = beside(*[nn(at, comb(ref, b)) for b in range(cols2) for ref in (even_ref, odd_ref)])

        pl.when(core == 0)(lambda: attend(comb_own_ref, comb_far_ref))
        pl.when(core == 1)(lambda: attend(comb_far_ref, comb_own_ref))
        vhat, r = norm_parts(x_ref[...].astype(F32) + (acc_ref[...] + vec_ref[0:1]))
        vhat_ref[...] = vhat
        r_ref[...] = r
        normed_ref[...] = (vhat * vec_ref[1:2] + vec_ref[2:3]).astype(BF)
        acc_ref[...] = jnp.zeros_like(acc_ref)

    def forward(expd_ref, redu_ref, hid_ref):
        pre = nn(normed_ref[...], expd_ref[...].reshape(width, -1)) + eb_ref[0]
        cdf = 0.5 * (1.0 + lax.erf(pre * 0.7071067811865476))
        hidden = (pre * cdf).astype(BF)
        hid_ref[pl.ds(y, 1)] = hidden[None]
        slope = cdf + pre * (jnp.exp(-0.5 * pre * pre) * 0.3989422804014327)
        slope_ref[pl.ds(c, 1)] = slope[None]
        acc_ref[...] += nt(hidden, redu_ref[...].reshape(width, -1))

    pl.when((phase == 0) & (k == 0))(lambda: forward(expd_own_ref, redu_own_ref, hid_here_ref))
    pl.when((phase == 0) & (k == 1))(lambda: forward(expd_far_ref, redu_far_ref, hid_away_ref))

    @pl.when((phase == 0) & (c == cols - 1))
    def _():
        vhat, r = norm_parts(normed_ref[...].astype(F32) + (acc_ref[...] + vec_ref[3:4]))
        out_ref[...] = (vhat * vec_ref[4:5] + vec_ref[5:6]).astype(BF)
        dy = cot_ref[...].astype(F32)
        gf = norm_pull(dy, vhat, r, vec_ref[4:5])
        gf_ref[...] = gf
        sg = gf.astype(BF)
        shrink_ref[...] = sg
        sums_ref[0:1] = down(dy * vhat)
        sums_ref[1:2] = down(dy)
        sums_ref[5:6] = down(sg.astype(F32))
        acc_ref[...] = jnp.zeros_like(acc_ref)

    def backward(expd_ref, redu_ref, pre_ref, ebg_ref):
        hidden_grad = nn(shrink_ref[...], redu_ref[...].reshape(width, -1))
        pre_grad = (hidden_grad * slope_ref[pl.ds(c, 1)][0]).astype(BF)
        pre_ref[pl.ds(y, 1)] = pre_grad[None]
        ebg_ref[pl.ds(y, 1)] = down(pre_grad.astype(F32))[None]
        acc_ref[...] += nt(pre_grad, expd_ref[...].reshape(width, -1))

    pl.when((phase == 1) & (k == 0))(lambda: backward(expd_own_ref, redu_own_ref, pre_here_ref, ebg_here_ref))
    pl.when((phase == 1) & (k == 1))(lambda: backward(expd_far_ref, redu_far_ref, pre_away_ref, ebg_away_ref))

    @pl.when((phase == 1) & (c == cols - 1))
    def _():
        dy = gf_ref[...] + acc_ref[...]
        vhat = vhat_ref[...]
        resid = norm_pull(dy, vhat, r_ref[...], vec_ref[1:2])
        resid_ref[...] = resid
        bg = resid.astype(BF)
        sums_ref[2:3] = down(dy * vhat)
        sums_ref[3:4] = down(dy)
        sums_ref[4:5] = down(bg.astype(F32))

        def share(even_ref, odd_ref):
            for b in range(2 * cols2):
                (even_ref, odd_ref)[b % 2][b // 2] = bg[:, b * step : (b + 1) * step]

        pl.when(core == 0)(lambda: share(bg_here_ref, bg_away_ref))
        pl.when(core == 1)(lambda: share(bg_away_ref, bg_here_ref))
        da = jnp.zeros(acc_ref.shape, F32)
        for b in range(cols2):
            da = da + nt(bg_here_ref[b], comb(comb_own_ref, b)) + nt(bg_away_ref[b], comb(comb_far_ref, b))
        acc_ref[...] = da
        tot_ref[...] = jnp.zeros_like(tot_ref)
        back = back_ref[...]
        for p in range(pairs):
            here = slice(p * lanes, (p + 1) * lanes)
            st, total = pair_sums(msg_ref, p, pairs, feats, per)
            dq, state_grad, total_grad = query_back_pair(
                scale, acc_ref[:, here], a_ref[:, here], rd_ref[:, here], fq_ref[p], st, total, q_ref[:, here], back
            )
            dq_ref[:, here] = dq
            msg_out_ref[p * feats : (p + 1) * feats] = state_grad
            row_to_rows(tot_ref, p * per, total_grad)
        put_totals(msg_out_ref, tot_ref, pairs * feats)


def stacked(values, count):
    return jnp.concatenate([values] * count, axis=0)


def grad_cols_kernel(row_n, idx_ref, lh, lf, rh, rf, *refs):
    *vals, here_ref, away_ref = refs
    k = pl.program_id(0)
    half = pl.num_programs(0)
    for out_ref, bit in ((here_ref, idx_ref[1]), (away_ref, 1 - idx_ref[1])):
        at = pl.ds(bit * half + k, 1)
        grad = tn(lh[...], rh[at][0]) + tn(lf[...], rf[at][0])
        if vals:
            grad = beside(grad, stacked(vals[0][at][0], row_n))
        out_ref[0] = grad.astype(BF)


def grad_rows_kernel(row_n, idx_ref, lh_ref, lf_ref, rh_ref, rf_ref, here_ref, away_ref, scr_ref):
    grad = tn(lh_ref[...], rh_ref[0]) + tn(lf_ref[...], rf_ref[0])
    scr_ref[...] = grad.astype(BF).reshape(scr_ref.shape)
    b = idx_ref[2]
    for z in range(row_n // 2):
        here_ref[0, z] = scr_ref[2 * z + b]
        away_ref[0, z] = scr_ref[2 * z + 1 - b]


def flat_rows(row, lanes, rows):
    count = -(-row.shape[1] // lanes)
    row = beside(row, jnp.zeros((1, count * lanes - row.shape[1]), F32)) if row.shape[1] % lanes else row
    parts = [row[:, k * lanes : (k + 1) * lanes] for k in range(count)]
    return jnp.concatenate(parts + [jnp.zeros((rows - count, lanes), F32)], axis=0)


def grad_project_kernel(row_n, cut, n, idx_ref, lh_ref, lf_ref, rh_ref, rf_ref, ha_ref, aa_ref, hb_ref, ab_ref, scr_ref):
    y = pl.program_id(0)
    half = pl.num_programs(0) // 2
    rh, rf = rh_ref[0], rf_ref[0]
    grad = tn(lh_ref[...], rh) + tn(lf_ref[...], rf)
    first = grad[:, :cut].astype(BF)
    mine = lax.div(y, half) == idx_ref[1]
    k = lax.rem(y, half)

    @pl.when(mine)
    def _():
        ha_ref[pl.ds(k, 1)] = first[None]

    @pl.when(jnp.logical_not(mine))
    def _():
        aa_ref[pl.ds(k, 1)] = first[None]

    _, i_rows, lanes = scr_ref.shape
    bias = (down(rh.astype(F32)) + down(rf.astype(F32)))[:, :n]
    side = stacked(flat_rows(bias, lanes - (n - cut), i_rows), row_n)
    scr_ref[...] = beside(grad[:, cut:n], side).astype(BF).reshape(scr_ref.shape)
    b = idx_ref[2]
    for z in range(row_n // 2):
        hb_ref[0, z] = scr_ref[2 * z + b]
        ab_ref[0, z] = scr_ref[2 * z + 1 - b]


def on_device(
    inputs,
    cotangent,
    projector,
    projector_bias,
    combiner,
    combiner_bias,
    attend_gain,
    attend_shift,
    expander,
    expander_bias,
    reducer,
    reducer_bias,
    final_gain,
    final_shift,
    projection,
    lengths,
):
    row_n, col_n = lax.axis_size("row"), lax.axis_size("col")
    row_i, col_i = lax.axis_index("row"), lax.axis_index("col")
    mesh_axes = ("row", "col")
    micro, tok, width = inputs.shape
    feats, head = projection.shape
    i_rows, n_proj = projector.shape
    n_exp, n_com = expander.shape[1], combiner.shape[1]
    assert lengths.shape[0] == micro and col_n % micro == 0 and width % (2 * head) == 0
    assert col_n & (col_n - 1) == 0 and row_n & (row_n - 1) == 0
    sub = col_n // micro
    pairs = width // (2 * head)
    lanes = 2 * head
    tokens = micro * tok
    cols2 = col_n // 2
    scale = float(head) ** -0.25
    weight = float(feats) ** -0.5
    token_groups = [[g + sub * j for j in range(micro)] for g in range(sub)]
    seq_groups = [[r * col_n + j * sub + g for r in range(row_n) for g in range(sub)] for j in range(micro)]
    seq_n = row_n * sub

    def tie(values, *after):
        return lax.optimization_barrier((values, after))[0]

    def sds(shape, dtype):
        return jax.ShapeDtypeStruct(shape, dtype)

    def whole(array):
        rank = len(array.shape)
        return pl.BlockSpec(array.shape, lambda *g: (0,) * rank)

    def lead(array):
        rank = len(array.shape)
        return pl.BlockSpec((1,) + array.shape[1:], lambda y: (y,) + (0,) * (rank - 1))

    smem = pl.BlockSpec(memory_space=pltpu.SMEM)

    def kernel(name, body, args, outs, grid=(1,), in_specs=None, out_specs=None, scratch=(), vmem=58):
        return pl.pallas_call(
            body,
            grid=grid,
            in_specs=in_specs or [smem if a.dtype == jnp.int32 else whole(a) for a in args],
            out_specs=out_specs or [whole(o) for o in outs],
            out_shape=outs,
            scratch_shapes=list(scratch),
            compiler_params=pltpu.CompilerParams(
                dimension_semantics=("arbitrary",) * len(grid), vmem_limit_bytes=vmem * MIB
            ),
            name=name,
        )(*args)

    def gate(values, after):
        return pl.pallas_call(
            lambda values_ref, after_ref, out_ref: None,
            in_specs=[pl.BlockSpec(memory_space=pl.ANY)] * 2,
            out_specs=pl.BlockSpec(memory_space=pl.ANY),
            out_shape=sds(values.shape, values.dtype),
            input_output_aliases={0: 0},
            name="gate",
        )(values, after)

    def to_seq(blocks):
        return lax.all_to_all(
            blocks, "col", split_axis=0, concat_axis=0, tiled=True, axis_index_groups=token_groups
        )

    def seq_a2a(rows):
        return lax.all_to_all(
            rows, mesh_axes, split_axis=0, concat_axis=0, tiled=True, axis_index_groups=seq_groups
        )

    def flip(values, axis, bit):
        mask = bit * (col_n if axis == "row" else 1)
        return lax.ppermute(values, mesh_axes, [(d, d ^ mask) for d in range(row_n * col_n)])

    def bit_of(axis, bit):
        return (lax.axis_index(axis) // bit) % 2

    col_bits = [("col", 1 << k) for k in reversed(range(1, (col_n - 1).bit_length()))]
    row_bits = [("row", 1 << k) for k in reversed(range((row_n - 1).bit_length()))]
    all_bits = col_bits + row_bits
    order_a = col_bits + row_bits[::-1]
    order_b = row_bits[-1:] + col_bits + row_bits[:-1]
    core_bit = ("col", 1)
    core = bit_of(*core_bit)
    index = jnp.stack([core, bit_of(*col_bits[0]), bit_of(*row_bits[-1])]).astype(jnp.int32)

    def spread(block, order, live=()):
        live = list(live)
        for name in order:
            live = [n for n in all_bits if n in live or n == name]
            d = live.index(name)
            other = flip(block, *name)
            block = jnp.where(
                bit_of(*name) == 0, jnp.stack([block, other], axis=d), jnp.stack([other, block], axis=d)
            )
        return block, live

    def pad_lanes(a, n):
        return jnp.pad(a, ((0, 0), (0, n - a.shape[1])))

    cut = lanes_up(n_proj // 2)
    block, live = spread(projector, row_bits[:-1])
    part_a = spread(block[..., :cut], row_bits[-1:] + col_bits, live)[0].reshape(cols2, width, -1)
    part_b = spread(block[..., cut:], col_bits + row_bits[-1:], live)[0].reshape(cols2, width, -1)
    proj_bias = spread(projector_bias.astype(F32), col_bits)[0].reshape(cols2, 1, -1)
    expd_bias = spread(expander_bias.astype(F32), col_bits)[0].reshape(cols2, 1, -1)
    expd_bias = jnp.stack([expd_bias, flip(expd_bias, *core_bit)], axis=1).reshape(col_n, 1, -1)

    n_expd, n_comb = lanes_up(n_exp), lanes_up(n_com)
    packed = jnp.concatenate(
        [pad_lanes(expander, n_expd), pad_lanes(reducer.T, n_expd), pad_lanes(combiner, n_comb)], axis=1
    )
    core_groups = [[r * col_n + 2 * y + k for y in range(cols2) for r in range(row_n)] for k in range(2)]
    later = lax.all_gather(packed, mesh_axes, axis=0, tiled=True, axis_index_groups=core_groups)
    arrived = to_seq(jnp.concatenate([inputs, cotangent], axis=1))
    x, cot = (a.reshape(tokens, width) for a in (arrived[:, :tok], arrived[:, tok:]))
    x_far = flip(x, *core_bit)
    seq_id = col_i // sub
    slot = (row_i * col_n + col_i % sub + sub * jnp.arange(micro, dtype=jnp.int32))[:, None] * tok + jnp.arange(
        tok, dtype=jnp.int32
    )
    keep = (slot.reshape(tokens, 1) < lengths[seq_id]).astype(F32)
    keep = jnp.broadcast_to(keep, (tokens, lanes))

    omega_t = projection.T * scale
    high = lax.reduce_precision(omega_t, 8, 7)
    rest = (omega_t - high).astype(BF)
    high = high.astype(BF)
    none = jnp.zeros_like(high)
    rhs = jnp.concatenate([beside(high, none), beside(none, high), beside(rest, none), beside(none, rest)], axis=0)
    omega = projection.astype(BF)
    ones = jnp.ones_like(omega)
    blank = jnp.zeros_like(omega)
    back = jnp.concatenate([beside(omega, blank, ones, blank), beside(blank, omega, blank, ones)], axis=0)
    vec = jnp.stack([combiner_bias, attend_gain, attend_shift, reducer_bias, final_gain, final_shift])
    ebias = jnp.pad(expd_bias, ((0, 0), (0, 0), (0, n_expd - n_exp)))

    tw = (tokens, width)
    n_pad = lanes_up(n_proj)
    own = sds((cols2, tokens, n_pad), BF)
    proj_bias = jnp.pad(proj_bias, ((0, 0), (0, 0), (0, n_pad - n_proj)))
    here, away = kernel(
        "project",
        project_kernel,
        (x, x_far, part_a, part_b, proj_bias),
        [own, own],
        grid=(cols2,),
        in_specs=[whole(x), whole(x_far), lead(part_a), lead(part_b), lead(proj_bias)],
        out_specs=[lead(own), lead(own)],
    )
    far = flip(away, *core_bit)

    tot_rows = pairs * 2 * feats // lanes
    tot_rows = -(-tot_rows // 16) * 16
    used = pairs * feats + tot_rows
    msg_rows = -(-used // (16 * seq_n)) * 16 * seq_n
    part_rows = msg_rows // seq_n
    msg_shape = sds((msg_rows, lanes), BF)
    feat_shape = sds((pairs, tokens, 2 * feats), BF)
    tot_scratch = pltpu.VMEM((msg_rows - pairs * feats, lanes), F32)

    def reduce_part(arrived):
        mine = jnp.sum(arrived.reshape(seq_n, part_rows, lanes).astype(F32), axis=0).astype(BF)
        return jnp.tile(mine, (seq_n, 1))

    mixed, fq, fk, msg = kernel(
        "features",
        lambda *refs: features_kernel(scale, weight, n_proj, *refs),
        (index, here, far, rhs, keep),
        [sds((tokens, 3 * width), BF), feat_shape, feat_shape, msg_shape],
        scratch=[tot_scratch],
    )
    parts = reduce_part(seq_a2a(msg))
    state = seq_a2a(parts)
    later = gate(later, parts)
    later_far = flip(later, *core_bit).reshape(cols2 * row_n, i_rows, -1)
    later = later.reshape(cols2 * row_n, i_rows, -1)
    def fixed(shape):
        return pl.BlockSpec(shape, lambda p, c: (0,) * len(shape))

    half_shape = (cols2, tokens, n_expd)
    comb_shape = (cols2, tokens, n_com)
    outs = [
        sds(tw, BF),
        sds(tw, BF),
        sds(tw, BF),
        sds(half_shape, BF),
        sds(half_shape, BF),
        sds(half_shape, BF),
        sds(half_shape, BF),
        sds(tw, BF),
        sds(comb_shape, BF),
        sds(comb_shape, BF),
        sds(tw, F32),
        sds((8, width), F32),
        sds((cols2, 1, n_expd), F32),
        sds((cols2, 1, n_expd), F32),
        sds(tw, BF),
        msg_shape,
    ]

    def weight_spec(n, place):
        return pl.BlockSpec((row_n, i_rows, n), lambda p, c: (c // 2, 0, place))

    comb_spec = pl.BlockSpec((cols2 * row_n, i_rows, n_comb), lambda p, c: (0, 0, 2 * n_expd // n_comb))
    (
        attended,
        layer_out,
        normed,
        hid_here,
        hid_away,
        pre_here,
        pre_away,
        shrink_grad,
        bg_here,
        bg_away,
        resid_grad,
        sums,
        ebg_here,
        ebg_away,
        dq,
        msg,
    ) = kernel(
        "middle",
        lambda *refs: middle_kernel(scale, *refs),
        (index, fq, state, mixed, back, x, cot, vec, ebias) + (later, later_far) * 3,
        outs,
        grid=(2, col_n),
        in_specs=[
            smem,
            fixed(fq.shape),
            fixed(state.shape),
            fixed(tw),
            fixed(back.shape),
            fixed(tw),
            fixed(tw),
            fixed(vec.shape),
            pl.BlockSpec((1, 1, n_expd), lambda p, c: (c, 0, 0)),
            comb_spec,
            comb_spec,
            weight_spec(n_expd, 0),
            weight_spec(n_expd, 0),
            weight_spec(n_expd, 1),
            weight_spec(n_expd, 1),
        ],
        out_specs=[fixed(o.shape) for o in outs],
        scratch=[
            pltpu.VMEM(tw, F32),
            pltpu.VMEM(tw, F32),
            pltpu.VMEM((tokens, 1), F32),
            pltpu.VMEM(tw, F32),
            pltpu.VMEM((col_n, tokens, n_expd), F32),
            pltpu.VMEM(tw, F32),
            pltpu.VMEM(tw, F32),
            tot_scratch,
        ],
        vmem=58,
    )

    arrived = seq_a2a(msg)

    def rounded(a):
        return lax.reduce_precision(a, 8, 7).astype(BF)

    class Stream:
        def __init__(self, order, here, away):
            self.order = list(order)
            self.live = [n for n in all_bits if n != order[0]]
            self.here, self.away = (a.reshape(-1, i_rows, a.shape[-1]) for a in (here, away))

        def send(self):
            self.got = flip(self.away, *self.order.pop(0))

        def hold(self, *after):
            self.got = tie(self.got, *after)

        def split(self):
            name = self.order[0]
            d = self.live.index(name)
            b = bit_of(*name)
            blocks, _, n = self.here.shape
            view = (1 << d, 2, (blocks >> (d + 1)) * i_rows, n)
            here, got = self.here.reshape(view), self.got.reshape(view)

            def side(bit):
                a, g = (lax.dynamic_index_in_dim(v, bit, 1, keepdims=False) for v in (here, got))
                return rounded(a.astype(F32) + g.astype(F32)).reshape(blocks // 2, i_rows, n)

            self.away, self.here = side(1 - b), side(b)
            self.live.remove(name)

        def last(self):
            return (self.here.astype(F32) + self.got.astype(F32)).reshape(i_rows, -1)

    (
        normed,
        shrink_grad,
        attended,
        hid_here,
        hid_away,
        pre_here,
        pre_away,
        bg_here,
        bg_away,
        ebg_here,
        ebg_away,
        sums,
    ) = tie(
        (
            normed,
            shrink_grad,
            attended,
            hid_here,
            hid_away,
            pre_here,
            pre_away,
            bg_here,
            bg_away,
            ebg_here,
            ebg_away,
            sums,
        ),
        msg,
    )
    hid_far, pre_far, bg_far = (flip(a, *core_bit) for a in (hid_away, pre_away, bg_away))
    shrink_far, normed_far, attended_far = (flip(a, *core_bit) for a in (shrink_grad, normed, attended))
    small = jnp.tile(sums[:6].reshape(1, -1), (cols2, 1))
    small_here = beside(ebg_here.reshape(cols2, -1), small)
    small_here = small_here + flip(beside(ebg_away.reshape(cols2, -1), small), *core_bit)
    count = small_here.shape[1]
    extra = lanes_up(n_com + -(-count // i_rows)) - n_com
    small_here = jnp.pad(small_here, ((0, 0), (0, i_rows * extra - count))).reshape(cols2, i_rows, extra)

    row_out = sds((cols2, row_n // 2, i_rows, n_expd), BF)

    def grad_cols(name, left, left_far, right, right_far, *vals):
        out = sds((cols2 // 2, width, right.shape[-1] + sum(v.shape[-1] for v in vals)), BF)
        return kernel(
            name,
            lambda *refs: grad_cols_kernel(row_n, *refs),
            (index, left, left_far, right, right_far) + vals,
            [out, out],
            grid=(cols2 // 2,),
            out_specs=[lead(out), lead(out)],
        )

    expd_s = Stream(
        order_b,
        *kernel(
            "expander_grad",
            lambda *refs: grad_rows_kernel(row_n, *refs),
            (index, normed, normed_far, pre_here, pre_far),
            [row_out, row_out],
            grid=(cols2,),
            in_specs=[smem, whole(normed), whole(normed_far), lead(pre_here), lead(pre_far)],
            out_specs=[lead(row_out), lead(row_out)],
            scratch=[pltpu.VMEM((row_n, i_rows, n_expd), BF)],
        ),
    )
    redu_s = Stream(order_a, *grad_cols("reducer_grad", shrink_grad, shrink_far, hid_here, hid_far))
    comb_s = Stream(order_a, *grad_cols("combiner_grad", attended, attended_far, bg_here, bg_far, small_here))
    expd_s.send()
    redu_s.send()
    comb_s.send()
    parts = reduce_part(tie(arrived, redu_s.away, expd_s.away))
    state_grad = seq_a2a(parts)
    streams = (expd_s, redu_s, comb_s)
    for s in streams:
        s.hold(parts)
        s.split()
        s.send()
    state_grad = tie(state_grad, *[s.away for s in streams])

    grad_here, grad_away = kernel(
        "key_back",
        lambda *refs: key_back_kernel(scale, n_proj, *refs),
        (index, fk, state_grad, mixed, dq, back),
        [own, own],
        scratch=[pltpu.VMEM((tokens, 3 * width), BF)],
    )
    grad_far = flip(grad_away, *core_bit)
    n_side = lanes_up(n_proj - cut + -(-n_proj // i_rows))
    out_a = sds((cols2 // 2, width, cut), BF)
    out_b = sds((cols2, row_n // 2, i_rows, n_side), BF)
    here_a, away_a, here_b, away_b = kernel(
        "projector_grad",
        lambda *refs: grad_project_kernel(row_n, cut, n_proj, *refs),
        (index, x, x_far, grad_here, grad_far),
        [out_a, out_a, out_b, out_b],
        grid=(cols2,),
        in_specs=[smem, whole(x), whole(x_far), lead(grad_here), lead(grad_far)],
        out_specs=[whole(out_a), whole(out_a), lead(out_b), lead(out_b)],
        scratch=[pltpu.VMEM((row_n, i_rows, n_side), BF)],
    )
    proj_s = (Stream(order_a, here_a, away_a), Stream(order_b, here_b, away_b))
    for s in proj_s:
        s.send()

    def advance(group, *after):
        done = list(after)
        for s in group:
            s.hold(*done)
            s.split()
            s.send()
            done = [s.away]
        return done[0]

    last = advance(proj_s, advance(streams, away_a, away_b))
    gh, gf = tie((grad_here, grad_far), last)
    mine, other = kernel(
        "project_back",
        project_back_kernel,
        (gh, gf, part_a, part_b, resid_grad),
        [sds(tw, F32), sds(tw, BF)],
        grid=(cols2,),
        in_specs=[lead(gh), lead(gf), lead(part_a), lead(part_b), whole(resid_grad)],
        scratch=[pltpu.VMEM(tw, F32)],
    )
    other_far = flip(other, *core_bit)
    last = other
    for _ in range(len(all_bits) - 3):
        last = advance(proj_s, advance(streams, last))
    input_grad = (mine + tie(other_far, last).astype(F32)).astype(BF).reshape(micro, tok, width)
    sent = to_seq(jnp.concatenate([layer_out.reshape(micro, tok, width), input_grad], axis=1))
    layer_out, input_grad = sent[:, :tok], sent[:, tok:].astype(F32)
    last = advance(proj_s, last)
    for s in streams:
        s.hold(last)
    expd_grad, redu_grad, comb_grad = (s.last() for s in streams)
    proj_grad = jnp.concatenate([s.last() for s in proj_s], axis=-1)

    pb = proj_grad[:, n_proj:].reshape(-1)[:n_proj]
    small = comb_grad[:, n_com:].reshape(-1)
    vec = [small[n_expd + i * width : n_expd + (i + 1) * width] for i in range(6)]
    return (
        layer_out,
        input_grad,
        proj_grad[:, :n_proj],
        pb,
        comb_grad[:, :n_com],
        vec[4],
        vec[2],
        vec[3],
        expd_grad[:, :n_exp],
        small[:n_exp],
        redu_grad[:, :n_exp].T,
        vec[5],
        vec[0],
        vec[1],
    )


def solution(mesh):
    placed = (
        P(None, ("row", "col"), None),
        P(None, ("row", "col"), None),
        P("row", "col"),
        P("col"),
        P("row", "col"),
        P(),
        P(),
        P(),
        P("row", "col"),
        P("col"),
        P("col", "row"),
        P(),
        P(),
        P(),
        P(),
        P(),
    )
    return jax.shard_map(
        on_device,
        mesh=mesh,
        in_specs=placed,
        out_specs=(
            P(None, ("row", "col"), None),
            P(None, ("row", "col"), None),
            P("row", "col"),
            P("col"),
            P("row", "col"),
            P(),
            P(),
            P(),
            P("row", "col"),
            P("col"),
            P("col", "row"),
            P(),
            P(),
            P(),
        ),
        check_vma=False,
    )
```

time: 1900 us -> 302 us (0.16)
  waiting for transfers between devices: 1380 us -> 87.4 us
  blocking collectives: 192 us -> 30.3 us
  matrix products: 133 us -> 0 us
  Pallas kernels: 0 us -> 59.2 us
  local copies, waits for them, and re-layouts: 79.4 us -> 21.7 us
  other arithmetic: 58.1 us -> 23.8 us
  starting transfers between devices: 30.6 us -> 63.2 us
    unnamed x48 -> x1, waiting for transfers between devices: 585 us -> 0.02 us
    reduce_scatter x24 -> x0, waiting for transfers between devices: 485 us -> none  [the longest x4 264 us: reduce_grads(): lax.psum_scatter(reduce_sum.astype(jnp.bfloat16), 'row', scatter_dimensio...]
    psum x3 -> x0, waiting for transfers between devices: 290 us -> none  [the longest x2 230 us: micro_step(): lax.psum((slot_four * state_grad[None], slot_three * total_grad[None], sm...]
    all_gather x14 -> x0, blocking collectives: 152 us -> none  [the longest x1 34.7 us: fetch_weights(): lax.all_gather(project_cols, 'row', axis=0, tiled=True)]
    dot_general x96 -> x0, matrix products: 133 us -> none  [the longest x16 27.8 us: contract_rows(): lax.dot_general(left_mat, right_mat, (((0,), (0,)), ((), ())), preferred_...]
    ppermute x0 -> x41, waiting for transfers between devices: none -> 72 us  [flip(): lax.ppermute(values, mesh_axes, [(d, d ^ mask) for d in range(row_n * col...]
    pallas_call x0 -> x10, Pallas kernels: none -> 59.2 us  [the longest x9 59.2 us: kernel(): pl.pallas_call(body, grid=grid, in_specs=in_specs or [smem if a.dtype ==...]
    ppermute x0 -> x41, starting transfers between devices: none -> 44.1 us  [flip(): lax.ppermute(values, mesh_axes, [(d, d ^ mask) for d in range(row_n * col...]
  transfers between devices with their start and end apart: 47 -> 47, of which waited for: 32 -> 16; matrix products, arithmetic and copies ran while one was open for 11% -> 12% of each run, Pallas kernels for 0% -> 10%
where the time goes in v1:
time: 302 us; the launch traced here: 300 us
  waiting for transfers between devices  87.4 us (29%)
  starting transfers between devices  63.2 us (21%)
  Pallas kernels  59.2 us (20%)
  blocking collectives  30.3 us (10%)
  other arithmetic  23.8 us (8%)
  local copies, waits for them, and re-layouts  21.7 us (7%)
  between operations  14.7 us (5%)
    ppermute x41, waiting for transfers between devices, flip(): lax.ppermute(values, mesh_axes, [(d, d ^ mask) for d in range(row_n * col...  72 us
    pallas_call x9, Pallas kernels, kernel(): pl.pallas_call(body, grid=grid, in_specs=in_specs or [smem if a.dtype ==...  59.2 us
    ppermute x41, starting transfers between devices, flip(): lax.ppermute(values, mesh_axes, [(d, d ^ mask) for d in range(row_n * col...  44.1 us
    all_to_all x1, blocking collectives, seq_a2a(): lax.all_to_all(rows, mesh_axes, split_axis=0, concat_axis=0, tiled=True,...  30.3 us
    all_to_all x3, starting transfers between devices, seq_a2a(): lax.all_to_all(rows, mesh_axes, split_axis=0, concat_axis=0, tiled=True,...  12 us
    all_gather x1, waiting for transfers between devices, on_device(): lax.all_gather(packed, mesh_axes, axis=0, tiled=True, axis_index_groups=c...  8.27 us
    all_to_all x2, starting transfers between devices, to_seq(): lax.all_to_all(blocks, 'col', split_axis=0, concat_axis=0, tiled=True, ax...  7.12 us
    unnamed x75, local copies, waits for them, and re-layouts  7.09 us
  transfers between devices with their start and end apart: 47, of which 16 were waited for; matrix products, arithmetic and copies ran while one was open for 12% of the time, Pallas kernels for 10%

profile of v1, /device:TPU:0, one launch (start us, length us, event | category | flops | bytes accessed | tf_op | source)
XLA Modules:
  0.0 300.3 jit_solution(16311490020111808590)
XLA Ops:
  9.1 4.1 %collective-permute-start.1 = (bf16[96,576]{1,0:T(8,128)(2,1)}, bf16[96,576]{1,0:T(8,128)(2,1)S(1)}, u32[]{:S(2)}, u32[]{:S(2)}) collective-permute-start(bf16[96,576]{1,0:T(8,128)(2,1)} %param.18), channel_id=1, source_target_pairs={{0,16},{1,17},{2,18},{3,19},{4,20},{5,21},{6,22},{7,23},{8,24},{9,... | collective-permute-start | bytes 331784 | tf_op jit(solution)/shard_map/ppermute | solution.py:513
  13.2 6.2 %collective-permute-done.1 = bf16[96,576]{1,0:T(8,128)(2,1)S(1)} collective-permute-done((bf16[96,576]{1,0:T(8,128)(2,1)}, bf16[96,576]{1,0:T(8,128)(2,1)S(1)}, u32[]{:S(2)}, u32[]{:S(2)}) %collective-permute-start.1) | collective-permute-done | bytes 110624 | tf_op jit(solution)/shard_map/ppermute | solution.py:513
  21.3 3.5 %all-to-all-start = ((bf16[4,128,768]{2,1,0:T(8,128)(2,1)}), bf16[4,128,768]{2,1,0:T(8,128)(2,1)S(1)}, u32[]{:S(2)}, u32[]{:S(2)}) async-start(bf16[4,128,768]{2,1,0:T(8,128)(2,1)} %pad_maximum_fusion), calls=%async_computation | async-start | bytes 1572864 | tf_op jit(solution)/shard_map/all_to_all | solution.py:502
  33.4 3.6 %collective-permute-done.7 = f32[576]{0:T(1024)S(1)} collective-permute-done((f32[576]{0:T(1024)S(1)}, f32[576]{0:T(1024)S(1)}, u32[]{:S(2)}, u32[]{:S(2)}) %collective-permute-start.7) | collective-permute-done | bytes 2336 | tf_op jit(solution)/shard_map/ppermute | solution.py:513
  45.4 15.7 %collective-permute-done.6 = bf16[2,2,2,96,192]{4,3,2,1,0:T(8,128)(2,1)S(1)} collective-permute-done((bf16[2,2,2,96,192]{4,3,2,1,0:T(8,128)(2,1)}, bf16[2,2,2,96,192]{4,3,2,1,0:T(8,128)(2,1)S(1)}, u32[]{:S(2)}, u32[]{:S(2)}) %collective-permute-start.6) | collective-permute-done | bytes 294944 | tf_op jit(solution)/shard_map/ppermute | solution.py:513
  65.4 4.0 %project.1 = (bf16[2,256,640]{2,1,0:T(8,128)(2,1)}, bf16[2,256,640]{2,1,0:T(8,128)(2,1)}) custom-call(bf16[256,768]{1,0:T(8,128)(2,1)} %bitcast.144, bf16[256,768]{1,0:T(8,128)(2,1)} %copy-done.4, bf16[2,768,384]{2,1,0:T(8,128)(2,1)} %maximum_select_fusion.pa_ref, bf16[2,768,192]{2,1,0:T(8,128)(2,1)} %bitcast.141, f32[2,1,640]{2,1,0:T(1,128)} %pad.16.bias_ref), custom_call_target="tpu_custom_call" | custom-call | tf_op jit(solution)/shard_map/project/pallas_call | solution.py:478
  72.6 6.2 %features.1 = (bf16[256,2304]{1,0:T(8,128)(2,1)}, bf16[6,256,512]{2,1,0:T(8,128)(2,1)}, bf16[6,256,512]{2,1,0:T(8,128)(2,1)}, bf16[1664,128]{1,0:T(8,128)(2,1)}) custom-call(s32[3]{0:T(128)} %pad_add_fusion.refs_0_, bf16[2,256,640]{2,1,0:T(8,128)(2,1)} %get-tuple-element.85.refs_1_, bf16[2,256,640]{2,1,0:T(8,128)(2,1)} %copy-done.11, ...), custom_call_target="tpu_custom_call" | custom-call | tf_op jit(solution)/shard_map/features/pallas_call | solution.py:478
  78.8 30.3 %all_to_all.48 = bf16[8,208,128]{2,1,0:T(8,128)(2,1)S(1)} all-to-all(bf16[8,208,128]{2,1,0:T(8,128)(2,1)} %bitcast.176), channel_id=1, replica_groups={{0,4,8,12,16,20,24,28},{1,5,9,13,17,21,25,29},{2,6,10,14,18,22,26,30},{..., dimensions={0} | all-to-all | bytes 851968 | tf_op jit(solution)/shard_map/all_to_all | solution.py:507
  109.2 8.3 %all-gather.2.cloned.1.call-done.values_ref = bf16[1536,1792]{1,0:T(8,128)(2,1)} async-done(((bf16[96,1792]{1,0:T(8,128)(2,1)}), bf16[1536,1792]{1,0:T(8,128)(2,1)}) %all-gather.2.cloned.1.call-update) | async-done | bytes 5505040 | tf_op jit(solution)/shard_map/all_gather | solution.py:554
  118.4 3.7 %all-to-all-start.2 = ((bf16[8,208,128]{2,1,0:T(8,128)(2,1)}), bf16[8,208,128]{2,1,0:T(8,128)(2,1)S(1)}, u32[]{:S(2)}, u32[]{:S(2)}) async-start(bf16[8,208,128]{2,1,0:T(8,128)(2,1)} %tile.12), calls=%async_computation.2 | async-start | bytes 851968 | tf_op jit(solution)/shard_map/all_to_all | solution.py:507
  128.0 7.1 %all-to-all-done.2 = bf16[8,208,128]{2,1,0:T(8,128)(2,1)S(1)} async-done(((bf16[8,208,128]{2,1,0:T(8,128)(2,1)}), bf16[8,208,128]{2,1,0:T(8,128)(2,1)S(1)}, u32[]{:S(2)}, u32[]{:S(2)}) %all-to-all-start.2) | async-done | bytes 426016 | tf_op jit(solution)/shard_map/all_to_all | solution.py:507
  135.9 23.9 %middle.1 = (bf16[256,768]{1,0:T(8,128)(2,1)}, bf16[256,768]{1,0:T(8,128)(2,1)}, bf16[256,768]{1,0:T(8,128)(2,1)}, bf16[2,256,768]{2,1,0:T(8,128)(2,1)}, bf16[2,...) custom-call(s32[3]{0:T(128)} %pad_add_fusion.refs_0_, ...), custom_call_target="tpu_custom_call" | custom-call | tf_op jit(solution)/shard_map/middle/pallas_call | solution.py:478
  163.0 3.7 %all-to-all-start.3 = ((bf16[8,208,128]{2,1,0:T(8,128)(2,1)}), bf16[8,208,128]{2,1,0:T(8,128)(2,1)S(1)}, u32[]{:S(2)}, u32[]{:S(2)}) async-start(bf16[8,208,128]{2,1,0:T(8,128)(2,1)} %bitcast.175), calls=%async_computation.3 | async-start | bytes 851968 | tf_op jit(solution)/shard_map/all_to_all | solution.py:507
  168.8 4.2 %expander_grad.1 = (bf16[2,4,96,768]{3,2,1,0:T(8,128)(2,1)}, bf16[2,4,96,768]{3,2,1,0:T(8,128)(2,1)}) custom-call(s32[3]{0:T(128)} %pad_add_fusion.refs_0_, bf16[256,768]{1,0:T(8,128)(2,1)} %get-tuple-element.109.refs_1_, bf16[256,768]{1,0:T(8,128)(2,1)} %copy-done.15, bf16[2,256,768]{2,1,0:T(8,128)(2,1)} %get-tuple-element.110.refs_3_, ...), custom_call_target="tpu_custom_call" | custom-call | tf_op jit(solution)/shard_map/expander_grad/pallas_call | solution.py:478
  175.6 4.1 %reducer_grad.1 = (bf16[1,768,768]{2,1,0:T(8,128)(2,1)}, bf16[1,768,768]{2,1,0:T(8,128)(2,1)}) custom-call(s32[3]{0:T(128)} %pad_add_fusion.refs_0_, bf16[256,768]{1,0:T(8,128)(2,1)} %get-tuple-element.105.refs_1_, bf16[256,768]{1,0:T(8,128)(2,1)} %copy-done.14, bf16[2,256,768]{2,1,0:T(8,128)(2,1)} %get-tuple-element.106.refs_3_, bf16[2,256,768]{2,1,0:T(8,128)(2,1)} %copy-done.7), custom_call_target="tpu_custom_call" | custom-call | tf_op jit(solution)/shard_map/reducer_grad/pallas_call | solution.py:478
  187.0 4.6 %all-to-all-start.4 = ((bf16[8,208,128]{2,1,0:T(8,128)(2,1)}), bf16[8,208,128]{2,1,0:T(8,128)(2,1)S(1)}, u32[]{:S(2)}, u32[]{:S(2)}) async-start(bf16[8,208,128]{2,1,0:T(8,128)(2,1)} %tile.28), calls=%async_computation.4 | async-start | bytes 851968 | tf_op jit(solution)/shard_map/all_to_all | solution.py:507
  191.7 24.8 %collective-permute-done.21 = bf16[8,96,256]{2,1,0:T(8,128)(2,1)} collective-permute-done((bf16[8,96,256]{2,1,0:T(8,128)(2,1)}, bf16[8,96,256]{2,1,0:T(8,128)(2,1)}, u32[]{:S(2)}, u32[]{:S(2)}) %collective-permute-start.21) | collective-permute-done | bytes 393248 | tf_op jit(solution)/shard_map/ppermute | solution.py:513
  222.7 5.1 %key_back.1 = (bf16[2,256,640]{2,1,0:T(8,128)(2,1)}, bf16[2,256,640]{2,1,0:T(8,128)(2,1)}) custom-call(s32[3]{0:T(128)} %pad_add_fusion.refs_0_, bf16[6,256,512]{2,1,0:T(8,128)(2,1)} %get-tuple-element.91.refs_1_, bf16[1664,128]{1,0:T(8,128)(2,1)} %bitcast.151, bf16[256,2304]{1,0:T(8,128)(2,1)} %get-tuple-element.89.refs_3_, ...), custom_call_target="tpu_custom_call" | custom-call | tf_op jit(solution)/shard_map/key_back/pallas_call | solution.py:478
  231.1 4.5 %projector_grad.1 = (bf16[1,768,384]{2,1,0:T(8,128)(2,1)}, bf16[1,768,384]{2,1,0:T(8,128)(2,1)}, bf16[2,4,96,256]{3,2,1,0:T(8,128)(2,1)}, bf16[2,4,96,256]{3,2,1,0:T(8,128)(2,1)}) custom-call(s32[3]{0:T(128)} %pad_add_fusion.refs_0_, bf16[256,768]{1,0:T(8,128)(2,1)} %bitcast.146, bf16[256,768]{1,0:T(8,128)(2,1)} %copy-done.4, ...), custom_call_target="tpu_custom_call" | custom-call | tf_op jit(solution)/shard_map/projector_grad/pallas_call | solution.py:478
  239.0 5.2 %collective-permute-done.27 = bf16[4,96,768]{2,1,0:T(8,128)(2,1)S(1)} collective-permute-done((bf16[4,96,768]{2,1,0:T(8,128)(2,1)}, bf16[4,96,768]{2,1,0:T(8,128)(2,1)S(1)}, u32[]{:S(2)}, u32[]{:S(2)}) %collective-permute-start.27) | collective-permute-done | bytes 589856 | tf_op jit(solution)/shard_map/ppermute | solution.py:513
  251.5 4.9 %collective-permute-done.24 = bf16[8,96,384]{2,1,0:T(8,128)(2,1)S(1)} collective-permute-done((bf16[8,96,384]{2,1,0:T(8,128)(2,1)}, bf16[8,96,384]{2,1,0:T(8,128)(2,1)S(1)}, u32[]{:S(2)}, u32[]{:S(2)}) %collective-permute-start.24) | collective-permute-done | bytes 589856 | tf_op jit(solution)/shard_map/ppermute | solution.py:513
  259.2 4.5 %project_back.1 = (f32[256,768]{1,0:T(8,128)}, bf16[256,768]{1,0:T(8,128)(2,1)}) custom-call(bf16[2,256,640]{2,1,0:T(8,128)(2,1)} %get-tuple-element.140.refs_3_.gh_ref, bf16[2,256,640]{2,1,0:T(8,128)(2,1)} %copy-done.1, bf16[2,768,384]{2,1,0:T(8,128)(2,1)} %maximum_select_fusion.pa_ref, bf16[2,768,192]{2,1,0:T(8,128)(2,1)} %bitcast.142, ...), custom_call_target="tpu_custom_call" | custom-call | tf_op jit(solution)/shard_map/project_back/pallas_call | solution.py:478
  272.7 3.6 %all-to-all-start.5 = ((bf16[4,128,768]{2,1,0:T(8,128)(2,1)}), bf16[4,128,768]{2,1,0:T(8,128)(2,1)S(1)}, u32[]{:S(2)}, u32[]{:S(2)}) async-start(bf16[4,128,768]{2,1,0:T(8,128)(2,1)} %pad_maximum_fusion.1), calls=%async_computation.5 | async-start | bytes 1572864 | tf_op jit(solution)/shard_map/all_to_all | solution.py:502
  276.9 3.5 %collective-permute-start.35 = (bf16[1,96,384]{2,1,0:T(8,128)(2,1)S(1)}, bf16[1,96,384]{2,1,0:T(8,128)(2,1)S(1)}, u32[]{:S(2)}, u32[]{:S(2)}) collective-permute-start(bf16[1,96,384]{2,1,0:T(8,128)(2,1)S(1)} %fusion.25), channel_id=1, source_target_pairs={{0,16},{1,17},{2,18},{3,19},{4,20},{5,21},{6,22},{7,23},{8,24},{9,... | collective-permute-start | bytes 221192 | tf_op jit(solution)/shard_map/ppermute | solution.py:513
  (249 shorter events, 96.4 us)
Async XLA Ops:
  7.2 110.2 %all-gather.2.cloned.1.call-start = ((), (), s32[]{:S(2)}) async-start(), calls=%async_computation.6 | async-start | bytes 5849088 | tf_op jit(solution)/shard_map/all_gather | solution.py:554
  21.3 22.5 %all-to-all-start = ((bf16[4,128,768]{2,1,0:T(8,128)(2,1)}), bf16[4,128,768]{2,1,0:T(8,128)(2,1)S(1)}, u32[]{:S(2)}, u32[]{:S(2)}) async-start(bf16[4,128,768]{2,1,0:T(8,128)(2,1)} %pad_maximum_fusion), calls=%async_computation | async-start | bytes 1572864 | tf_op jit(solution)/shard_map/all_to_all | solution.py:502
  41.6 19.5 %collective-permute-start.6 = (bf16[2,2,2,96,192]{4,3,2,1,0:T(8,128)(2,1)}, bf16[2,2,2,96,192]{4,3,2,1,0:T(8,128)(2,1)S(1)}, u32[]{:S(2)}, u32[]{:S(2)}) collective-permute-start(bf16[2,2,2,96,192]{4,3,2,1,0:T(8,128)(2,1)} %maximum_select_fusion.6), channel_id=1, source_target_pairs={{0,4},{1,5},{2,6},{3,7},{4,0},{5,1},{6,2},{7,3},{8,12},{9,13},{10,... | collective-permute-start | bytes 884744 | tf_op jit(solution)/shard_map/ppermute | solution.py:513
  43.2 19.0 %collective-permute-start.4 = (bf16[2,2,2,96,384]{4,3,1,0,2:T(8,128)(2,1)S(1)}, bf16[2,2,2,96,384]{4,3,1,0,2:T(8,128)(2,1)}, u32[]{:S(2)}, u32[]{:S(2)}) collective-permute-start(bf16[2,2,2,96,384]{4,3,1,0,2:T(8,128)(2,1)S(1)} %maximum_select_fusion.3), channel_id=1, source_target_pairs={{0,2},{1,3},{2,0},{3,1},{4,6},{5,7},{6,4},{7,5},{8,10},{9,11},{10,... | collective-permute-start | bytes 1769480 | tf_op jit(solution)/shard_map/ppermute | solution.py:513
  44.6 20.0 %collective-permute-start = (bf16[256,768]{1,0:T(8,128)(2,1)S(1)}, bf16[256,768]{1,0:T(8,128)(2,1)S(1)}, u32[]{:S(2)}, u32[]{:S(2)}) collective-permute-start(bf16[256,768]{1,0:T(8,128)(2,1)S(1)} %bitcast.143), channel_id=1, source_target_pairs={{0,1},{1,0},{2,3},{3,2},{4,5},{5,4},{6,7},{7,6},{8,9},{9,8},{10,11... | collective-permute-start | bytes 1179656 | tf_op jit(solution)/shard_map/ppermute | solution.py:513
  118.3 16.8 %collective-permute-start.11 = (bf16[1536,1792]{1,0:T(8,128)(2,1)}, bf16[1536,1792]{1,0:T(8,128)(2,1)}, u32[]{:S(2)}, u32[]{:S(2)}) collective-permute-start(bf16[1536,1792]{1,0:T(8,128)(2,1)} %gate.1), channel_id=1, source_target_pairs={{0,1},{1,0},{2,3},{3,2},{4,5},{5,4},{6,7},{7,6},{8,9},{9,8},{10,11... | collective-permute-start | bytes 16515080 | tf_op jit(solution)/shard_map/ppermute | solution.py:513
  118.4 16.7 %all-to-all-start.2 = ((bf16[8,208,128]{2,1,0:T(8,128)(2,1)}), bf16[8,208,128]{2,1,0:T(8,128)(2,1)S(1)}, u32[]{:S(2)}, u32[]{:S(2)}) async-start(bf16[8,208,128]{2,1,0:T(8,128)(2,1)} %tile.12), calls=%async_computation.2 | async-start | bytes 851968 | tf_op jit(solution)/shard_map/all_to_all | solution.py:507
  163.0 18.2 %collective-permute-start.20 = (f32[2,5376]{1,0:T(2,128)}, f32[2,5376]{1,0:T(2,128)}, u32[]{:S(2)}, u32[]{:S(2)}) collective-permute-start(f32[2,5376]{1,0:T(2,128)} %pad_maximum_fusion.3), channel_id=1, source_target_pairs={{0,1},{1,0},{2,3},{3,2},{4,5},{5,4},{6,7},{7,6},{8,9},{9,8},{10,11... | collective-permute-start | bytes 129032 | tf_op jit(solution)/shard_map/ppermute | solution.py:513
  163.0 23.1 %all-to-all-start.3 = ((bf16[8,208,128]{2,1,0:T(8,128)(2,1)}), bf16[8,208,128]{2,1,0:T(8,128)(2,1)S(1)}, u32[]{:S(2)}, u32[]{:S(2)}) async-start(bf16[8,208,128]{2,1,0:T(8,128)(2,1)} %bitcast.175), calls=%async_computation.3 | async-start | bytes 851968 | tf_op jit(solution)/shard_map/all_to_all | solution.py:507
  167.4 15.3 %collective-permute-start.18 = (bf16[256,768]{1,0:T(8,128)(2,1)}, bf16[256,768]{1,0:T(8,128)(2,1)}, u32[]{:S(2)}, u32[]{:S(2)}) collective-permute-start(bf16[256,768]{1,0:T(8,128)(2,1)} %get-tuple-element.118.refs_1_), channel_id=1, source_target_pairs={{0,1},{1,0},{2,3},{3,2},{4,5},{5,4},{6,7},{7,6},{8,9},{9,8},{10,11... | collective-permute-start | bytes 1179656 | tf_op jit(solution)/shard_map/ppermute | solution.py:513
  173.0 45.3 %collective-permute-start.16 = (bf16[8,96,768]{2,1,0:T(8,128)(2,1)}, bf16[8,96,768]{2,1,0:T(8,128)(2,1)S(1)}, u32[]{:S(2)}, u32[]{:S(2)}) collective-permute-start(bf16[8,96,768]{2,1,0:T(8,128)(2,1)} %bitcast.198), channel_id=1, source_target_pairs={{0,4},{1,5},{2,6},{3,7},{4,0},{5,1},{6,2},{7,3},{8,12},{9,13},{10,... | collective-permute-start | bytes 3538952 | tf_op jit(solution)/shard_map/ppermute | solution.py:513
  179.7 38.7 %collective-permute-start.17 = (bf16[8,96,768]{2,1,0:T(8,128)(2,1)}, bf16[8,96,768]{2,1,0:T(8,128)(2,1)}, u32[]{:S(2)}, u32[]{:S(2)}) collective-permute-start(bf16[8,96,768]{2,1,0:T(8,128)(2,1)} %bitcast.199), channel_id=1, source_target_pairs={{0,2},{1,3},{2,0},{3,1},{4,6},{5,7},{6,4},{7,5},{8,10},{9,11},{10,... | collective-permute-start | bytes 3538952 | tf_op jit(solution)/shard_map/ppermute | solution.py:513
  185.6 30.9 %collective-permute-start.21 = (bf16[8,96,256]{2,1,0:T(8,128)(2,1)}, bf16[8,96,256]{2,1,0:T(8,128)(2,1)}, u32[]{:S(2)}, u32[]{:S(2)}) collective-permute-start(bf16[8,96,256]{2,1,0:T(8,128)(2,1)} %bitcast.202), channel_id=1, source_target_pairs={{0,2},{1,3},{2,0},{3,1},{4,6},{5,7},{6,4},{7,5},{8,10},{9,11},{10,... | collective-permute-start | bytes 1179656 | tf_op jit(solution)/shard_map/ppermute | solution.py:513
  187.0 34.9 %all-to-all-start.4 = ((bf16[8,208,128]{2,1,0:T(8,128)(2,1)}), bf16[8,208,128]{2,1,0:T(8,128)(2,1)S(1)}, u32[]{:S(2)}, u32[]{:S(2)}) async-start(bf16[8,208,128]{2,1,0:T(8,128)(2,1)} %tile.28), calls=%async_computation.4 | async-start | bytes 851968 | tf_op jit(solution)/shard_map/all_to_all | solution.py:507
  227.8 16.3 %collective-permute-start.27 = (bf16[4,96,768]{2,1,0:T(8,128)(2,1)}, bf16[4,96,768]{2,1,0:T(8,128)(2,1)S(1)}, u32[]{:S(2)}, u32[]{:S(2)}) collective-permute-start(bf16[4,96,768]{2,1,0:T(8,128)(2,1)} %bitcast.42), channel_id=1, source_target_pairs={{0,2},{1,3},{2,0},{3,1},{4,6},{5,7},{6,4},{7,5},{8,10},{9,11},{10,... | collective-permute-start | bytes 1769480 | tf_op jit(solution)/shard_map/ppermute | solution.py:513
  229.3 17.4 %collective-permute-start.26 = (bf16[4,96,768]{2,1,0:T(8,128)(2,1)}, bf16[4,96,768]{2,1,0:T(8,128)(2,1)S(1)}, u32[]{:S(2)}, u32[]{:S(2)}) collective-permute-start(bf16[4,96,768]{2,1,0:T(8,128)(2,1)} %get-tuple-element.157), channel_id=1, source_target_pairs={{0,4},{1,5},{2,6},{3,7},{4,0},{5,1},{6,2},{7,3},{8,12},{9,13},{10,... | collective-permute-start | bytes 1769480 | tf_op jit(solution)/shard_map/ppermute | solution.py:513
  235.6 20.8 %collective-permute-start.24 = (bf16[8,96,384]{2,1,0:T(8,128)(2,1)}, bf16[8,96,384]{2,1,0:T(8,128)(2,1)S(1)}, u32[]{:S(2)}, u32[]{:S(2)}) collective-permute-start(bf16[8,96,384]{2,1,0:T(8,128)(2,1)} %bitcast.200), channel_id=1, source_target_pairs={{0,2},{1,3},{2,0},{3,1},{4,6},{5,7},{6,4},{7,5},{8,10},{9,11},{10,... | collective-permute-start | bytes 1769480 | tf_op jit(solution)/shard_map/ppermute | solution.py:513
  237.9 19.7 %collective-permute-start.23 = (bf16[8,96,256]{2,1,0:T(8,128)(2,1)}, bf16[8,96,256]{2,1,0:T(8,128)(2,1)S(1)}, u32[]{:S(2)}, u32[]{:S(2)}) collective-permute-start(bf16[8,96,256]{2,1,0:T(8,128)(2,1)} %bitcast.201), channel_id=1, source_target_pairs={{0,4},{1,5},{2,6},{3,7},{4,0},{5,1},{6,2},{7,3},{8,12},{9,13},{10,... | collective-permute-start | bytes 1179656 | tf_op jit(solution)/shard_map/ppermute | solution.py:513
  244.3 19.4 %collective-permute-start.33 = (bf16[2,96,768]{2,1,0:T(8,128)(2,1)S(1)}, bf16[2,96,768]{2,1,0:T(8,128)(2,1)S(1)}, u32[]{:S(2)}, u32[]{:S(2)}) collective-permute-start(bf16[2,96,768]{2,1,0:T(8,128)(2,1)S(1)} %bitcast.184), channel_id=1, source_target_pairs={{0,16},{1,17},{2,18},{3,19},{4,20},{5,21},{6,22},{7,23},{8,24},{9,... | collective-permute-start | bytes 884744 | tf_op jit(solution)/shard_map/ppermute | solution.py:513
  246.9 16.9 %collective-permute-start.32 = (bf16[2,96,768]{2,1,0:T(8,128)(2,1)S(1)}, bf16[2,96,768]{2,1,0:T(8,128)(2,1)S(1)}, u32[]{:S(2)}, u32[]{:S(2)}) collective-permute-start(bf16[2,96,768]{2,1,0:T(8,128)(2,1)S(1)} %get-tuple-element.163), channel_id=1, source_target_pairs={{0,8},{1,9},{2,10},{3,11},{4,12},{5,13},{6,14},{7,15},{8,0},{9,1},... | collective-permute-start | bytes 884744 | tf_op jit(solution)/shard_map/ppermute | solution.py:513
  249.9 15.4 %collective-permute-start.31 = (bf16[2,96,256]{2,1,0:T(8,128)(2,1)S(1)}, bf16[2,96,256]{2,1,0:T(8,128)(2,1)S(1)}, u32[]{:S(2)}, u32[]{:S(2)}) collective-permute-start(bf16[2,96,256]{2,1,0:T(8,128)(2,1)S(1)} %get-tuple-element.185), channel_id=1, source_target_pairs={{0,8},{1,9},{2,10},{3,11},{4,12},{5,13},{6,14},{7,15},{8,0},{9,1},... | collective-permute-start | bytes 294920 | tf_op jit(solution)/shard_map/ppermute | solution.py:513
  263.8 19.1 %collective-permute-start.39 = (bf16[1,96,768]{2,1,0:T(8,128)(2,1)S(1)}, bf16[1,96,768]{2,1,0:T(8,128)(2,1)S(1)}, u32[]{:S(2)}, u32[]{:S(2)}) collective-permute-start(bf16[1,96,768]{2,1,0:T(8,128)(2,1)S(1)} %fusion.16), channel_id=1, source_target_pairs={{0,8},{1,9},{2,10},{3,11},{4,12},{5,13},{6,14},{7,15},{8,0},{9,1},... | collective-permute-start | bytes 442376 | tf_op jit(solution)/shard_map/ppermute | solution.py:513
  265.4 19.1 %collective-permute-start.40 = (bf16[1,96,768]{2,1,0:T(8,128)(2,1)S(1)}, bf16[1,96,768]{2,1,0:T(8,128)(2,1)S(1)}, u32[]{:S(2)}, u32[]{:S(2)}) collective-permute-start(bf16[1,96,768]{2,1,0:T(8,128)(2,1)S(1)} %fusion.18), channel_id=1, source_target_pairs={{0,16},{1,17},{2,18},{3,19},{4,20},{5,21},{6,22},{7,23},{8,24},{9,... | collective-permute-start | bytes 442376 | tf_op jit(solution)/shard_map/ppermute | solution.py:513
  272.7 19.6 %all-to-all-start.5 = ((bf16[4,128,768]{2,1,0:T(8,128)(2,1)}), bf16[4,128,768]{2,1,0:T(8,128)(2,1)S(1)}, u32[]{:S(2)}, u32[]{:S(2)}) async-start(bf16[4,128,768]{2,1,0:T(8,128)(2,1)} %pad_maximum_fusion.1), calls=%async_computation.5 | async-start | bytes 1572864 | tf_op jit(solution)/shard_map/all_to_all | solution.py:502
  (59 other events, 467.3 us)
Sparse Core Ops, SparseCore 0:
  10.8 106.5 all-gather.1

commit v2 on v1

--- a/solution.py
+++ b/solution.py
@@ -291,12 +291,19 @@
         acc_ref[...] = jnp.zeros_like(acc_ref)
 
     def forward(expd_ref, redu_ref, hid_ref):
-        pre = nn(normed_ref[...], expd_ref[...].reshape(width, -1)) + eb_ref[0]
-        cdf = 0.5 * (1.0 + lax.erf(pre * 0.7071067811865476))
-        hidden = (pre * cdf).astype(BF)
+        expd, bias, normed = expd_ref[...].reshape(width, -1), eb_ref[0], normed_ref[...]
+        n = expd.shape[1]
+        wide = 256 if n % 256 == 0 else n
+        hidden = []
+        for j in range(0, n, wide):
+            cols_j = slice(j, j + wide)
+            pre = nn(normed, expd[:, cols_j]) + bias[:, cols_j]
+            cdf = 0.5 * (1.0 + lax.erf(pre * 0.7071067811865476))
+            hidden.append((pre * cdf).astype(BF))
+            slope = cdf + pre * (jnp.exp(-0.5 * pre * pre) * 0.3989422804014327)
+            slope_ref[pl.ds(c, 1), :, cols_j] = slope[None]
+        hidden = beside(*hidden)
         hid_ref[pl.ds(y, 1)] = hidden[None]
-        slope = cdf + pre * (jnp.exp(-0.5 * pre * pre) * 0.3989422804014327)
-        slope_ref[pl.ds(c, 1)] = slope[None]
         acc_ref[...] += nt(hidden, redu_ref[...].reshape(width, -1))
 
     pl.when((phase == 0) & (k == 0))(lambda: forward(expd_own_ref, redu_own_ref, hid_here_ref))
@@ -365,25 +372,29 @@
     return jnp.concatenate([values] * count, axis=0)
 
 
-def grad_cols_kernel(row_n, idx_ref, lh, lf, rh, rf, *refs):
-    *vals, here_ref, away_ref = refs
+def grad_cols_kernel(idx_ref, lh, lf, rh, rf, here_ref, away_ref):
     k = pl.program_id(0)
     half = pl.num_programs(0)
     for out_ref, bit in ((here_ref, idx_ref[1]), (away_ref, 1 - idx_ref[1])):
         at = pl.ds(bit * half + k, 1)
-        grad = tn(lh[...], rh[at][0]) + tn(lf[...], rf[at][0])
-        if vals:
-            grad = beside(grad, stacked(vals[0][at][0], row_n))
-        out_ref[0] = grad.astype(BF)
-
-
-def grad_rows_kernel(row_n, idx_ref, lh_ref, lf_ref, rh_ref, rf_ref, here_ref, away_ref, scr_ref):
+        out_ref[0] = (tn(lh[...], rh[at][0]) + tn(lf[...], rf[at][0])).astype(BF)
+
+
+def share_rows(scr_ref, place, b, here_ref, away_ref):
+    for n in range(scr_ref.shape[0] // 2):
+        low = n & ((1 << place) - 1)
+        r = ((n - low) << 1) + low
+        here_ref[0, n] = scr_ref[r + (b << place)]
+        away_ref[0, n] = scr_ref[r + ((1 - b) << place)]
+
+
+def grad_rows_kernel(place, idx_ref, lh_ref, lf_ref, rh_ref, rf_ref, *refs):
+    *vals, here_ref, away_ref, scr_ref = refs
     grad = tn(lh_ref[...], rh_ref[0]) + tn(lf_ref[...], rf_ref[0])
+    if vals:
+        grad = beside(grad, stacked(vals[0][0], scr_ref.shape[0]))
     scr_ref[...] = grad.astype(BF).reshape(scr_ref.shape)
-    b = idx_ref[2]
-    for z in range(row_n // 2):
-        here_ref[0, z] = scr_ref[2 * z + b]
-        away_ref[0, z] = scr_ref[2 * z + 1 - b]
+    share_rows(scr_ref, place, idx_ref[2 + place], here_ref, away_ref)
 
 
 def flat_rows(row, lanes, rows):
@@ -414,10 +425,21 @@
     bias = (down(rh.astype(F32)) + down(rf.astype(F32)))[:, :n]
     side = stacked(flat_rows(bias, lanes - (n - cut), i_rows), row_n)
     scr_ref[...] = beside(grad[:, cut:n], side).astype(BF).reshape(scr_ref.shape)
-    b = idx_ref[2]
-    for z in range(row_n // 2):
-        hb_ref[0, z] = scr_ref[2 * z + b]
-        ab_ref[0, z] = scr_ref[2 * z + 1 - b]
+    share_rows(scr_ref, 0, idx_ref[2], hb_ref, ab_ref)
+
+
+def row_of(values, first, count):
+    rows = [values[first + k : first + k + 1] for k in range(-(-count // values.shape[1]))]
+    return beside(*rows)[:, :count]
+
+
+def finish_kernel(firsts, here_ref, got_ref, grad_ref, *vec_refs):
+    total = here_ref[0].astype(F32) + got_ref[0].astype(F32)
+    n = grad_ref.shape[1]
+    grad_ref[...] = total[:, :n]
+    side = total[:, n:]
+    for first, ref in zip(firsts, vec_refs):
+        ref[...] = row_of(side, first, ref.shape[0])[0]
 
 
 def on_device(
@@ -522,7 +544,9 @@
     order_b = row_bits[-1:] + col_bits + row_bits[:-1]
     core_bit = ("col", 1)
     core = bit_of(*core_bit)
-    index = jnp.stack([core, bit_of(*col_bits[0]), bit_of(*row_bits[-1])]).astype(jnp.int32)
+    order_z = row_bits[:-1][::-1] + row_bits[-1:] + col_bits
+    order_x = row_bits[-1:] + row_bits[:-1][::-1] + col_bits
+    index = jnp.stack([core, bit_of(*col_bits[0])] + [bit_of(*n) for n in row_bits[::-1]]).astype(jnp.int32)
 
     def spread(block, order, live=()):
         live = list(live)
@@ -771,34 +795,36 @@
     extra = lanes_up(n_com + -(-count // i_rows)) - n_com
     small_here = jnp.pad(small_here, ((0, 0), (0, i_rows * extra - count))).reshape(cols2, i_rows, extra)
 
-    row_out = sds((cols2, row_n // 2, i_rows, n_expd), BF)
-
-    def grad_cols(name, left, left_far, right, right_far, *vals):
-        out = sds((cols2 // 2, width, right.shape[-1] + sum(v.shape[-1] for v in vals)), BF)
+    def grad_cols(name, left, left_far, right, right_far):
+        out = sds((cols2 // 2, width, right.shape[-1]), BF)
         return kernel(
             name,
-            lambda *refs: grad_cols_kernel(row_n, *refs),
-            (index, left, left_far, right, right_far) + vals,
+            grad_cols_kernel,
+            (index, left, left_far, right, right_far),
             [out, out],
             grid=(cols2 // 2,),
             out_specs=[lead(out), lead(out)],
         )
 
-    expd_s = Stream(
-        order_b,
-        *kernel(
-            "expander_grad",
-            lambda *refs: grad_rows_kernel(row_n, *refs),
-            (index, normed, normed_far, pre_here, pre_far),
-            [row_out, row_out],
+    def grad_rows(name, place, left, left_far, right, right_far, *vals):
+        n = right.shape[-1] + sum(v.shape[-1] for v in vals)
+        out = sds((cols2, row_n // 2, i_rows, n), BF)
+        return kernel(
+            name,
+            lambda *refs: grad_rows_kernel(place, *refs),
+            (index, left, left_far, right, right_far) + vals,
+            [out, out],
             grid=(cols2,),
-            in_specs=[smem, whole(normed), whole(normed_far), lead(pre_here), lead(pre_far)],
-            out_specs=[lead(row_out), lead(row_out)],
-            scratch=[pltpu.VMEM((row_n, i_rows, n_expd), BF)],
-        ),
-    )
+            in_specs=[smem, whole(left), whole(left_far)] + [lead(a) for a in (right, right_far) + vals],
+            out_specs=[lead(out), lead(out)],
+            scratch=[pltpu.VMEM((row_n, i_rows, n), BF)],
+        )
+
+    expd_s = Stream(order_x, *grad_rows("expander_grad", 0, normed, normed_far, pre_here, pre_far))
     redu_s = Stream(order_a, *grad_cols("reducer_grad", shrink_grad, shrink_far, hid_here, hid_far))
-    comb_s = Stream(order_a, *grad_cols("combiner_grad", attended, attended_far, bg_here, bg_far, small_here))
+    comb_s = Stream(
+        order_z, *grad_rows("combiner_grad", 1, attended, attended_far, bg_here, bg_far, small_here)
+    )
     expd_s.send()
     redu_s.send()
     comb_s.send()
@@ -845,7 +871,8 @@
             done = [s.away]
         return done[0]
 
-    last = advance(proj_s, advance(streams, away_a, away_b))
+    last = advance(proj_s, advance((expd_s, redu_s), away_a, away_b))
+    last = advance((comb_s,), last)
     gh, gf = tie((grad_here, grad_far), last)
     mine, other = kernel(
         "project_back",
@@ -859,30 +886,42 @@
     other_far = flip(other, *core_bit)
     last = other
     for _ in range(len(all_bits) - 3):
-        last = advance(proj_s, advance(streams, last))
+        last = advance(proj_s, advance((expd_s, redu_s), last))
+        last = advance((comb_s,), last)
     input_grad = (mine + tie(other_far, last).astype(F32)).astype(BF).reshape(micro, tok, width)
     sent = to_seq(jnp.concatenate([layer_out.reshape(micro, tok, width), input_grad], axis=1))
     layer_out, input_grad = sent[:, :tok], sent[:, tok:].astype(F32)
     last = advance(proj_s, last)
     for s in streams:
         s.hold(last)
-    expd_grad, redu_grad, comb_grad = (s.last() for s in streams)
+    expd_grad, redu_grad = expd_s.last(), redu_s.last()
     proj_grad = jnp.concatenate([s.last() for s in proj_s], axis=-1)
-
     pb = proj_grad[:, n_proj:].reshape(-1)[:n_proj]
-    small = comb_grad[:, n_com:].reshape(-1)
-    vec = [small[n_expd + i * width : n_expd + (i + 1) * width] for i in range(6)]
+    side = comb_s.here.shape[-1] - n_com
+    places = [0] + [n_expd + v * width for v in range(6)]
+    if all(place % side == 0 for place in places):
+        comb_grad, eb, *vec = kernel(
+            "finish",
+            lambda *refs: finish_kernel([place // side for place in places], *refs),
+            (comb_s.here, comb_s.got),
+            [sds((i_rows, n_com), F32), sds((n_exp,), F32)] + [sds((width,), F32)] * 6,
+        )
+    else:
+        comb_grad = comb_s.last()
+        small = comb_grad[:, n_com:].reshape(-1)
+        comb_grad, eb = comb_grad[:, :n_com], small[:n_exp]
+        vec = [small[place : place + width] for place in places[1:]]
     return (
         layer_out,
         input_grad,
         proj_grad[:, :n_proj],
         pb,
-        comb_grad[:, :n_com],
+        comb_grad,
         vec[4],
         vec[2],
         vec[3],
         expd_grad[:, :n_exp],
-        small[:n_exp],
+        eb,
         redu_grad[:, :n_exp].T,
         vec[5],
         vec[0],

time: 302 us -> 288 us (0.954)
  waiting for transfers between devices: 87.4 us -> 79.9 us
  starting transfers between devices: 63.2 us -> 59.2 us
    ppermute x41, waiting for transfers between devices: 72 us -> 62.6 us  [flip(): lax.ppermute(values, mesh_axes, [(d, d ^ mask) for d in range(row_n * col...]
    slice x8 -> x0, local copies, waits for them, and re-layouts: 4.71 us -> none  [the longest x7 4.05 us: on_device(): vec = [small[n_expd + i * width:n_expd + (i + 1) * width] for i in range(6)]]
    ppermute x41, starting transfers between devices: 44.1 us -> 40.1 us  [flip(): lax.ppermute(values, mesh_axes, [(d, d ^ mask) for d in range(row_n * col...]
    unnamed x75, local copies, waits for them, and re-layouts: 7.09 us -> 10.5 us
    pallas_call x9 -> x10, Pallas kernels: 59.2 us -> 60.9 us  [kernel(): pl.pallas_call(body, grid=grid, in_specs=in_specs or [smem if a.dtype ==...]
    convert_element_type x15 -> x14, other arithmetic: 6.88 us -> 8.32 us  [rounded(): return lax.reduce_precision(a, 8, 7).astype(BF)]
  transfers between devices with their start and end apart: 47 -> 47, of which waited for: 16 -> 19; matrix products, arithmetic and copies ran while one was open for 12% -> 11% of each run, Pallas kernels for 10% -> 11%
where the time goes in v2:
time: 288 us; the launch traced here: 287 us
  waiting for transfers between devices  79.9 us (28%)
  Pallas kernels  60.9 us (21%)
  starting transfers between devices  59.2 us (21%)
  blocking collectives  29.2 us (10%)
  other arithmetic  21.6 us (8%)
  local copies, waits for them, and re-layouts  21 us (7%)
  between operations  14.7 us (5%)
    ppermute x41, waiting for transfers between devices, flip(): lax.ppermute(values, mesh_axes, [(d, d ^ mask) for d in range(row_n * col...  62.6 us
    pallas_call x10, Pallas kernels, kernel(): pl.pallas_call(body, grid=grid, in_specs=in_specs or [smem if a.dtype ==...  60.9 us
    ppermute x41, starting transfers between devices, flip(): lax.ppermute(values, mesh_axes, [(d, d ^ mask) for d in range(row_n * col...  40.1 us
    all_to_all x1, blocking collectives, seq_a2a(): lax.all_to_all(rows, mesh_axes, split_axis=0, concat_axis=0, tiled=True,...  29.2 us
    all_to_all x3, starting transfers between devices, seq_a2a(): lax.all_to_all(rows, mesh_axes, split_axis=0, concat_axis=0, tiled=True,...  12 us
    unnamed x75, local copies, waits for them, and re-layouts  10.5 us
    all_gather x1, waiting for transfers between devices, on_device(): lax.all_gather(packed, mesh_axes, axis=0, tiled=True, axis_index_groups=c...  8.69 us
    convert_element_type x14, other arithmetic, rounded(): return lax.reduce_precision(a, 8, 7).astype(BF)  8.32 us
  transfers between devices with their start and end apart: 47, of which 19 were waited for; matrix products, arithmetic and copies ran while one was open for 11% of the time, Pallas kernels for 11%

profile of v2, /device:TPU:0, one launch (start us, length us, event | category | flops | bytes accessed | tf_op | source)
XLA Modules:
  0.0 286.6 jit_solution(2752714347235163822)
XLA Ops:
  9.1 4.1 %collective-permute-start.1 = (bf16[96,576]{1,0:T(8,128)(2,1)}, bf16[96,576]{1,0:T(8,128)(2,1)S(1)}, u32[]{:S(2)}, u32[]{:S(2)}) collective-permute-start(bf16[96,576]{1,0:T(8,128)(2,1)} %param.18), channel_id=1, source_target_pairs={{0,16},{1,17},{2,18},{3,19},{4,20},{5,21},{6,22},{7,23},{8,24},{9,... | collective-permute-start | bytes 331784 | tf_op jit(solution)/shard_map/ppermute | solution.py:535
  13.2 6.2 %collective-permute-done.1 = bf16[96,576]{1,0:T(8,128)(2,1)S(1)} collective-permute-done((bf16[96,576]{1,0:T(8,128)(2,1)}, bf16[96,576]{1,0:T(8,128)(2,1)S(1)}, u32[]{:S(2)}, u32[]{:S(2)}) %collective-permute-start.1) | collective-permute-done | bytes 110624 | tf_op jit(solution)/shard_map/ppermute | solution.py:535
  21.3 3.5 %all-to-all-start = ((bf16[4,128,768]{2,1,0:T(8,128)(2,1)}), bf16[4,128,768]{2,1,0:T(8,128)(2,1)S(1)}, u32[]{:S(2)}, u32[]{:S(2)}) async-start(bf16[4,128,768]{2,1,0:T(8,128)(2,1)} %pad_maximum_fusion), calls=%async_computation | async-start | bytes 1572864 | tf_op jit(solution)/shard_map/all_to_all | solution.py:524
  24.9 4.5 %collective-permute-done.2 = bf16[2,96,576]{2,1,0:T(8,128)(2,1)S(1)} collective-permute-done((bf16[2,96,576]{2,1,0:T(8,128)(2,1)S(1)}, bf16[2,96,576]{2,1,0:T(8,128)(2,1)S(1)}, u32[]{:S(2)}, u32[]{:S(2)}) %collective-permute-start.2) | collective-permute-done | bytes 221216 | tf_op jit(solution)/shard_map/ppermute | solution.py:535
  33.8 6.9 %collective-permute-done.7 = f32[576]{0:T(1024)S(1)} collective-permute-done((f32[576]{0:T(1024)S(1)}, f32[576]{0:T(1024)S(1)}, u32[]{:S(2)}, u32[]{:S(2)}) %collective-permute-start.7) | collective-permute-done | bytes 2336 | tf_op jit(solution)/shard_map/ppermute | solution.py:535
  46.0 16.2 %collective-permute-done.6 = bf16[2,2,2,96,192]{4,3,2,1,0:T(8,128)(2,1)S(1)} collective-permute-done((bf16[2,2,2,96,192]{4,3,2,1,0:T(8,128)(2,1)}, bf16[2,2,2,96,192]{4,3,2,1,0:T(8,128)(2,1)S(1)}, u32[]{:S(2)}, u32[]{:S(2)}) %collective-permute-start.6) | collective-permute-done | bytes 294944 | tf_op jit(solution)/shard_map/ppermute | solution.py:535
  66.5 4.0 %project.1 = (bf16[2,256,640]{2,1,0:T(8,128)(2,1)}, bf16[2,256,640]{2,1,0:T(8,128)(2,1)}) custom-call(bf16[256,768]{1,0:T(8,128)(2,1)} %bitcast.143, bf16[256,768]{1,0:T(8,128)(2,1)} %copy-done.4, bf16[2,768,384]{2,1,0:T(8,128)(2,1)} %maximum_select_fusion.pa_ref, bf16[2,768,192]{2,1,0:T(8,128)(2,1)} %bitcast.140, f32[2,1,640]{2,1,0:T(1,128)} %pad.16.bias_ref), custom_call_target="tpu_custom_call" | custom-call | tf_op jit(solution)/shard_map/project/pallas_call | solution.py:500
  73.7 6.2 %features.1 = (bf16[256,2304]{1,0:T(8,128)(2,1)}, bf16[6,256,512]{2,1,0:T(8,128)(2,1)}, bf16[6,256,512]{2,1,0:T(8,128)(2,1)}, bf16[1664,128]{1,0:T(8,128)(2,1)}) custom-call(s32[5]{0:T(128)} %stack.188.refs_0_.idx_ref, bf16[2,256,640]{2,1,0:T(8,128)(2,1)} %get-tuple-element.93.refs_1_, bf16[2,256,640]{2,1,0:T(8,128)(2,1)} %copy-done.12, ...), custom_call_target="tpu_custom_call" | custom-call | tf_op jit(solution)/shard_map/features/pallas_call | solution.py:500
  79.9 29.2 %all_to_all.48 = bf16[8,208,128]{2,1,0:T(8,128)(2,1)S(1)} all-to-all(bf16[8,208,128]{2,1,0:T(8,128)(2,1)} %bitcast.173), channel_id=1, replica_groups={{0,4,8,12,16,20,24,28},{1,5,9,13,17,21,25,29},{2,6,10,14,18,22,26,30},{..., dimensions={0} | all-to-all | bytes 851968 | tf_op jit(solution)/shard_map/all_to_all | solution.py:529
  109.1 8.7 %all-gather.2.cloned.1.call-done.values_ref = bf16[1536,1792]{1,0:T(8,128)(2,1)} async-done(((bf16[96,1792]{1,0:T(8,128)(2,1)}), bf16[1536,1792]{1,0:T(8,128)(2,1)}) %all-gather.2.cloned.1.call-update) | async-done | bytes 5505040 | tf_op jit(solution)/shard_map/all_gather | solution.py:578
  118.8 3.7 %all-to-all-start.2 = ((bf16[8,208,128]{2,1,0:T(8,128)(2,1)}), bf16[8,208,128]{2,1,0:T(8,128)(2,1)S(1)}, u32[]{:S(2)}, u32[]{:S(2)}) async-start(bf16[8,208,128]{2,1,0:T(8,128)(2,1)} %tile.12), calls=%async_computation.2 | async-start | bytes 851968 | tf_op jit(solution)/shard_map/all_to_all | solution.py:529
  128.4 7.1 %all-to-all-done.2 = bf16[8,208,128]{2,1,0:T(8,128)(2,1)S(1)} async-done(((bf16[8,208,128]{2,1,0:T(8,128)(2,1)}), bf16[8,208,128]{2,1,0:T(8,128)(2,1)S(1)}, u32[]{:S(2)}, u32[]{:S(2)}) %all-to-all-start.2) | async-done | bytes 426016 | tf_op jit(solution)/shard_map/all_to_all | solution.py:529
  136.2 23.9 %middle.1 = (bf16[256,768]{1,0:T(8,128)(2,1)}, bf16[256,768]{1,0:T(8,128)(2,1)}, bf16[256,768]{1,0:T(8,128)(2,1)}, bf16[2,256,768]{2,1,0:T(8,128)(2,1)}, bf16[2,...) custom-call(s32[5]{0:T(128)} %stack.188.refs_0_.idx_ref, ...), custom_call_target="tpu_custom_call" | custom-call | tf_op jit(solution)/shard_map/middle/pallas_call | solution.py:500
  160.2 3.7 %all-to-all-start.3 = ((bf16[8,208,128]{2,1,0:T(8,128)(2,1)}), bf16[8,208,128]{2,1,0:T(8,128)(2,1)S(1)}, u32[]{:S(2)}, u32[]{:S(2)}) async-start(bf16[8,208,128]{2,1,0:T(8,128)(2,1)} %bitcast.172), calls=%async_computation.3 | async-start | bytes 851968 | tf_op jit(solution)/shard_map/all_to_all | solution.py:529
  169.6 4.2 %expander_grad.1 = (bf16[2,4,96,768]{3,2,1,0:T(8,128)(2,1)}, bf16[2,4,96,768]{3,2,1,0:T(8,128)(2,1)}) custom-call(s32[5]{0:T(128)} %stack.188.refs_0_.idx_ref, bf16[256,768]{1,0:T(8,128)(2,1)} %get-tuple-element.117.refs_1_, bf16[256,768]{1,0:T(8,128)(2,1)} %copy-done.17, bf16[2,256,768]{2,1,0:T(8,128)(2,1)} %get-tuple-element.118.refs_3_, ...), custom_call_target="tpu_custom_call" | custom-call | tf_op jit(solution)/shard_map/expander_grad/pallas_call | solution.py:500
  176.6 4.1 %reducer_grad.1 = (bf16[1,768,768]{2,1,0:T(8,128)(2,1)}, bf16[1,768,768]{2,1,0:T(8,128)(2,1)}) custom-call(s32[5]{0:T(128)} %stack.188.refs_0_.idx_ref, bf16[256,768]{1,0:T(8,128)(2,1)} %get-tuple-element.113.lh, bf16[256,768]{1,0:T(8,128)(2,1)} %copy-done.16, bf16[2,256,768]{2,1,0:T(8,128)(2,1)} %get-tuple-element.114.rh, bf16[2,256,768]{2,1,0:T(8,128)(2,1)} %copy-done.8), custom_call_target="tpu_custom_call" | custom-call | tf_op jit(solution)/shard_map/reducer_grad/pallas_call | solution.py:500
  183.1 4.6 %all-to-all-start.4 = ((bf16[8,208,128]{2,1,0:T(8,128)(2,1)}), bf16[8,208,128]{2,1,0:T(8,128)(2,1)S(1)}, u32[]{:S(2)}, u32[]{:S(2)}) async-start(bf16[8,208,128]{2,1,0:T(8,128)(2,1)} %tile.28), calls=%async_computation.4 | async-start | bytes 851968 | tf_op jit(solution)/shard_map/all_to_all | solution.py:529
  195.1 10.8 %collective-permute-done.21 = bf16[8,96,256]{2,1,0:T(8,128)(2,1)S(1)} collective-permute-done((bf16[8,96,256]{2,1,0:T(8,128)(2,1)}, bf16[8,96,256]{2,1,0:T(8,128)(2,1)S(1)}, u32[]{:S(2)}, u32[]{:S(2)}) %collective-permute-start.21) | collective-permute-done | bytes 393248 | tf_op jit(solution)/shard_map/ppermute | solution.py:535
  208.8 3.3 %reduce-precision_convert_fusion = (bf16[4,1,96,768]{3,2,1,0:T(8,128)(2,1)S(1)}, bf16[4,96,768]{2,1,0:T(8,128)(2,1)}, bf16[4,96,768]{2,1,0:T(8,128)(2,1)}, bf16[4,1,96,768]{3,2,1,0:T(8,128)(2,1)S(1)}) fusion(bf16[4,2,96,768]{3,2,1,0:T(8,128)(2,1)} %bitcast.155, s32[]{:T(128)S(6)} %select_n.369, bf16[4,2,96,768]{3,2,1,0:T(8,128)(2,1)S(1)} %bitcast.154, ...), kind=kLoop, calls=%fused_computation.1 | loop fusion | flops 5898240 | bytes 7077904 | tf_op jit(solution)/shard_map/convert_element_type | solution.py:727
  212.9 5.1 %key_back.1 = (bf16[2,256,640]{2,1,0:T(8,128)(2,1)}, bf16[2,256,640]{2,1,0:T(8,128)(2,1)}) custom-call(s32[5]{0:T(128)} %stack.188.refs_0_.idx_ref, bf16[6,256,512]{2,1,0:T(8,128)(2,1)} %get-tuple-element.99.refs_1_, bf16[1664,128]{1,0:T(8,128)(2,1)} %bitcast.150, bf16[256,2304]{1,0:T(8,128)(2,1)} %get-tuple-element.97.refs_3_, ...), custom_call_target="tpu_custom_call" | custom-call | tf_op jit(solution)/shard_map/key_back/pallas_call | solution.py:500
  221.2 4.5 %projector_grad.1 = (bf16[1,768,384]{2,1,0:T(8,128)(2,1)}, bf16[1,768,384]{2,1,0:T(8,128)(2,1)}, bf16[2,4,96,256]{3,2,1,0:T(8,128)(2,1)}, bf16[2,4,96,256]{3,2,1,0:T(8,128)(2,1)}) custom-call(s32[5]{0:T(128)} %stack.188.refs_0_.idx_ref, bf16[256,768]{1,0:T(8,128)(2,1)} %bitcast.145, bf16[256,768]{1,0:T(8,128)(2,1)} %copy-done.4, ...), custom_call_target="tpu_custom_call" | custom-call | tf_op jit(solution)/shard_map/projector_grad/pallas_call | solution.py:500
  230.6 7.5 %collective-permute-done.27 = bf16[4,96,768]{2,1,0:T(8,128)(2,1)S(1)} collective-permute-done((bf16[4,96,768]{2,1,0:T(8,128)(2,1)}, bf16[4,96,768]{2,1,0:T(8,128)(2,1)S(1)}, u32[]{:S(2)}, u32[]{:S(2)}) %collective-permute-start.27) | collective-permute-done | bytes 589856 | tf_op jit(solution)/shard_map/ppermute | solution.py:535
  247.6 4.5 %project_back.1 = (f32[256,768]{1,0:T(8,128)}, bf16[256,768]{1,0:T(8,128)(2,1)}) custom-call(bf16[2,256,640]{2,1,0:T(8,128)(2,1)} %get-tuple-element.148.refs_3_.gh_ref, bf16[2,256,640]{2,1,0:T(8,128)(2,1)} %copy-done.1, bf16[2,768,384]{2,1,0:T(8,128)(2,1)} %maximum_select_fusion.pa_ref, bf16[2,768,192]{2,1,0:T(8,128)(2,1)} %bitcast.141, ...), custom_call_target="tpu_custom_call" | custom-call | tf_op jit(solution)/shard_map/project_back/pallas_call | solution.py:500
  263.5 3.5 %all-to-all-start.5 = ((bf16[4,128,768]{2,1,0:T(8,128)(2,1)}), bf16[4,128,768]{2,1,0:T(8,128)(2,1)S(1)}, u32[]{:S(2)}, u32[]{:S(2)}) async-start(bf16[4,128,768]{2,1,0:T(8,128)(2,1)} %pad_maximum_fusion.1), calls=%async_computation.5 | async-start | bytes 1572864 | tf_op jit(solution)/shard_map/all_to_all | solution.py:524
  (240 shorter events, 92.0 us)
Async XLA Ops:
  7.2 110.6 %all-gather.2.cloned.1.call-start = ((), (), s32[]{:S(2)}) async-start(), calls=%async_computation.6 | async-start | bytes 5849088 | tf_op jit(solution)/shard_map/all_gather | solution.py:578
  21.3 23.1 %all-to-all-start = ((bf16[4,128,768]{2,1,0:T(8,128)(2,1)}), bf16[4,128,768]{2,1,0:T(8,128)(2,1)S(1)}, u32[]{:S(2)}, u32[]{:S(2)}) async-start(bf16[4,128,768]{2,1,0:T(8,128)(2,1)} %pad_maximum_fusion), calls=%async_computation | async-start | bytes 1572864 | tf_op jit(solution)/shard_map/all_to_all | solution.py:524
  42.2 19.9 %collective-permute-start.6 = (bf16[2,2,2,96,192]{4,3,2,1,0:T(8,128)(2,1)}, bf16[2,2,2,96,192]{4,3,2,1,0:T(8,128)(2,1)S(1)}, u32[]{:S(2)}, u32[]{:S(2)}) collective-permute-start(bf16[2,2,2,96,192]{4,3,2,1,0:T(8,128)(2,1)} %maximum_select_fusion.6), channel_id=1, source_target_pairs={{0,4},{1,5},{2,6},{3,7},{4,0},{5,1},{6,2},{7,3},{8,12},{9,13},{10,... | collective-permute-start | bytes 884744 | tf_op jit(solution)/shard_map/ppermute | solution.py:535
  43.8 19.5 %collective-permute-start.4 = (bf16[2,2,2,96,384]{4,3,1,0,2:T(8,128)(2,1)S(1)}, bf16[2,2,2,96,384]{4,3,1,0,2:T(8,128)(2,1)}, u32[]{:S(2)}, u32[]{:S(2)}) collective-permute-start(bf16[2,2,2,96,384]{4,3,1,0,2:T(8,128)(2,1)S(1)} %maximum_select_fusion.3), channel_id=1, source_target_pairs={{0,2},{1,3},{2,0},{3,1},{4,6},{5,7},{6,4},{7,5},{8,10},{9,11},{10,... | collective-permute-start | bytes 1769480 | tf_op jit(solution)/shard_map/ppermute | solution.py:535
  45.2 20.5 %collective-permute-start = (bf16[256,768]{1,0:T(8,128)(2,1)S(1)}, bf16[256,768]{1,0:T(8,128)(2,1)S(1)}, u32[]{:S(2)}, u32[]{:S(2)}) collective-permute-start(bf16[256,768]{1,0:T(8,128)(2,1)S(1)} %bitcast.142), channel_id=1, source_target_pairs={{0,1},{1,0},{2,3},{3,2},{4,5},{5,4},{6,7},{7,6},{8,9},{9,8},{10,11... | collective-permute-start | bytes 1179656 | tf_op jit(solution)/shard_map/ppermute | solution.py:535
  118.7 16.8 %collective-permute-start.11 = (bf16[1536,1792]{1,0:T(8,128)(2,1)}, bf16[1536,1792]{1,0:T(8,128)(2,1)}, u32[]{:S(2)}, u32[]{:S(2)}) collective-permute-start(bf16[1536,1792]{1,0:T(8,128)(2,1)} %gate.1), channel_id=1, source_target_pairs={{0,1},{1,0},{2,3},{3,2},{4,5},{5,4},{6,7},{7,6},{8,9},{9,8},{10,11... | collective-permute-start | bytes 16515080 | tf_op jit(solution)/shard_map/ppermute | solution.py:535
  118.8 16.7 %all-to-all-start.2 = ((bf16[8,208,128]{2,1,0:T(8,128)(2,1)}), bf16[8,208,128]{2,1,0:T(8,128)(2,1)S(1)}, u32[]{:S(2)}, u32[]{:S(2)}) async-start(bf16[8,208,128]{2,1,0:T(8,128)(2,1)} %tile.12), calls=%async_computation.2 | async-start | bytes 851968 | tf_op jit(solution)/shard_map/all_to_all | solution.py:529
  160.2 22.0 %all-to-all-start.3 = ((bf16[8,208,128]{2,1,0:T(8,128)(2,1)}), bf16[8,208,128]{2,1,0:T(8,128)(2,1)S(1)}, u32[]{:S(2)}, u32[]{:S(2)}) async-start(bf16[8,208,128]{2,1,0:T(8,128)(2,1)} %bitcast.172), calls=%async_computation.3 | async-start | bytes 851968 | tf_op jit(solution)/shard_map/all_to_all | solution.py:529
  166.4 21.3 %collective-permute-start.20 = (f32[2,5376]{1,0:T(2,128)S(1)}, f32[2,5376]{1,0:T(2,128)S(1)}, u32[]{:S(2)}, u32[]{:S(2)}) collective-permute-start(f32[2,5376]{1,0:T(2,128)S(1)} %pad_maximum_fusion.3), channel_id=1, source_target_pairs={{0,1},{1,0},{2,3},{3,2},{4,5},{5,4},{6,7},{7,6},{8,9},{9,8},{10,11... | collective-permute-start | bytes 129032 | tf_op jit(solution)/shard_map/ppermute | solution.py:535
  167.9 20.7 %collective-permute-start.18 = (bf16[256,768]{1,0:T(8,128)(2,1)}, bf16[256,768]{1,0:T(8,128)(2,1)S(1)}, u32[]{:S(2)}, u32[]{:S(2)}) collective-permute-start(bf16[256,768]{1,0:T(8,128)(2,1)} %get-tuple-element.126.refs_1_), channel_id=1, source_target_pairs={{0,1},{1,0},{2,3},{3,2},{4,5},{5,4},{6,7},{7,6},{8,9},{9,8},{10,11... | collective-permute-start | bytes 1179656 | tf_op jit(solution)/shard_map/ppermute | solution.py:535
  168.7 19.9 %collective-permute-start.19 = (bf16[2,256,192]{2,1,0:T(8,128)(2,1)}, bf16[2,256,192]{2,1,0:T(8,128)(2,1)S(1)}, u32[]{:S(2)}, u32[]{:S(2)}) collective-permute-start(bf16[2,256,192]{2,1,0:T(8,128)(2,1)} %get-tuple-element.128), channel_id=1, source_target_pairs={{0,1},{1,0},{2,3},{3,2},{4,5},{5,4},{6,7},{7,6},{8,9},{9,8},{10,11... | collective-permute-start | bytes 589832 | tf_op jit(solution)/shard_map/ppermute | solution.py:535
  173.8 34.0 %collective-permute-start.16 = (bf16[8,96,768]{2,1,0:T(8,128)(2,1)}, bf16[8,96,768]{2,1,0:T(8,128)(2,1)S(1)}, u32[]{:S(2)}, u32[]{:S(2)}) collective-permute-start(bf16[8,96,768]{2,1,0:T(8,128)(2,1)} %bitcast.195), channel_id=1, source_target_pairs={{0,4},{1,5},{2,6},{3,7},{4,0},{5,1},{6,2},{7,3},{8,12},{9,13},{10,... | collective-permute-start | bytes 3538952 | tf_op jit(solution)/shard_map/ppermute | solution.py:535
  180.7 28.0 %collective-permute-start.17 = (bf16[8,96,768]{2,1,0:T(8,128)(2,1)}, bf16[8,96,768]{2,1,0:T(8,128)(2,1)}, u32[]{:S(2)}, u32[]{:S(2)}) collective-permute-start(bf16[8,96,768]{2,1,0:T(8,128)(2,1)} %bitcast.196), channel_id=1, source_target_pairs={{0,2},{1,3},{2,0},{3,1},{4,6},{5,7},{6,4},{7,5},{8,10},{9,11},{10,... | collective-permute-start | bytes 3538952 | tf_op jit(solution)/shard_map/ppermute | solution.py:535
  183.1 29.0 %all-to-all-start.4 = ((bf16[8,208,128]{2,1,0:T(8,128)(2,1)}), bf16[8,208,128]{2,1,0:T(8,128)(2,1)S(1)}, u32[]{:S(2)}, u32[]{:S(2)}) async-start(bf16[8,208,128]{2,1,0:T(8,128)(2,1)} %tile.28), calls=%async_computation.4 | async-start | bytes 851968 | tf_op jit(solution)/shard_map/all_to_all | solution.py:529
  218.0 20.2 %collective-permute-start.27 = (bf16[4,96,768]{2,1,0:T(8,128)(2,1)}, bf16[4,96,768]{2,1,0:T(8,128)(2,1)S(1)}, u32[]{:S(2)}, u32[]{:S(2)}) collective-permute-start(bf16[4,96,768]{2,1,0:T(8,128)(2,1)} %get-tuple-element.175), channel_id=1, source_target_pairs={{0,8},{1,9},{2,10},{3,11},{4,12},{5,13},{6,14},{7,15},{8,0},{9,1},... | collective-permute-start | bytes 1769480 | tf_op jit(solution)/shard_map/ppermute | solution.py:535
  219.4 20.8 %collective-permute-start.26 = (bf16[4,96,768]{2,1,0:T(8,128)(2,1)}, bf16[4,96,768]{2,1,0:T(8,128)(2,1)S(1)}, u32[]{:S(2)}, u32[]{:S(2)}) collective-permute-start(bf16[4,96,768]{2,1,0:T(8,128)(2,1)} %get-tuple-element.206), channel_id=1, source_target_pairs={{0,4},{1,5},{2,6},{3,7},{4,0},{5,1},{6,2},{7,3},{8,12},{9,13},{10,... | collective-permute-start | bytes 1769480 | tf_op jit(solution)/shard_map/ppermute | solution.py:535
  225.7 17.1 %collective-permute-start.25 = (bf16[8,96,384]{2,1,0:T(8,128)(2,1)}, bf16[8,96,384]{2,1,0:T(8,128)(2,1)S(1)}, u32[]{:S(2)}, u32[]{:S(2)}) collective-permute-start(bf16[8,96,384]{2,1,0:T(8,128)(2,1)} %bitcast.197), channel_id=1, source_target_pairs={{0,2},{1,3},{2,0},{3,1},{4,6},{5,7},{6,4},{7,5},{8,10},{9,11},{10,... | collective-permute-start | bytes 1769480 | tf_op jit(solution)/shard_map/ppermute | solution.py:535
  227.2 16.5 %collective-permute-start.24 = (bf16[8,96,256]{2,1,0:T(8,128)(2,1)}, bf16[8,96,256]{2,1,0:T(8,128)(2,1)S(1)}, u32[]{:S(2)}, u32[]{:S(2)}) collective-permute-start(bf16[8,96,256]{2,1,0:T(8,128)(2,1)} %bitcast.198), channel_id=1, source_target_pairs={{0,4},{1,5},{2,6},{3,7},{4,0},{5,1},{6,2},{7,3},{8,12},{9,13},{10,... | collective-permute-start | bytes 1179656 | tf_op jit(solution)/shard_map/ppermute | solution.py:535
  228.3 17.9 %collective-permute-start.23 = (bf16[4,96,256]{2,1,0:T(8,128)(2,1)}, bf16[4,96,256]{2,1,0:T(8,128)(2,1)S(1)}, u32[]{:S(2)}, u32[]{:S(2)}) collective-permute-start(bf16[4,96,256]{2,1,0:T(8,128)(2,1)} %bitcast.186), channel_id=1, source_target_pairs={{0,16},{1,17},{2,18},{3,19},{4,20},{5,21},{6,22},{7,23},{8,24},{9,... | collective-permute-start | bytes 589832 | tf_op jit(solution)/shard_map/ppermute | solution.py:535
  240.1 15.2 %collective-permute-start.33 = (bf16[2,96,768]{2,1,0:T(8,128)(2,1)S(1)}, bf16[2,96,768]{2,1,0:T(8,128)(2,1)S(1)}, u32[]{:S(2)}, u32[]{:S(2)}) collective-permute-start(bf16[2,96,768]{2,1,0:T(8,128)(2,1)S(1)} %get-tuple-element.181), channel_id=1, source_target_pairs={{0,16},{1,17},{2,18},{3,19},{4,20},{5,21},{6,22},{7,23},{8,24},{9,... | collective-permute-start | bytes 884744 | tf_op jit(solution)/shard_map/ppermute | solution.py:535
  240.4 15.3 %collective-permute-start.32 = (bf16[2,96,768]{2,1,0:T(8,128)(2,1)S(1)}, bf16[2,96,768]{2,1,0:T(8,128)(2,1)S(1)}, u32[]{:S(2)}, u32[]{:S(2)}) collective-permute-start(bf16[2,96,768]{2,1,0:T(8,128)(2,1)S(1)} %get-tuple-element.179), channel_id=1, source_target_pairs={{0,8},{1,9},{2,10},{3,11},{4,12},{5,13},{6,14},{7,15},{8,0},{9,1},... | collective-permute-start | bytes 884744 | tf_op jit(solution)/shard_map/ppermute | solution.py:535
  243.8 15.1 %collective-permute-start.30 = (bf16[4,96,256]{2,1,0:T(8,128)(2,1)S(1)}, bf16[4,96,256]{2,1,0:T(8,128)(2,1)S(1)}, u32[]{:S(2)}, u32[]{:S(2)}) collective-permute-start(bf16[4,96,256]{2,1,0:T(8,128)(2,1)S(1)} %bitcast.187), channel_id=1, source_target_pairs={{0,2},{1,3},{2,0},{3,1},{4,6},{5,7},{6,4},{7,5},{8,10},{9,11},{10,... | collective-permute-start | bytes 589832 | tf_op jit(solution)/shard_map/ppermute | solution.py:535
  255.7 15.7 %collective-permute-start.39 = (bf16[1,96,768]{2,1,0:T(8,128)(2,1)S(1)}, bf16[1,96,768]{2,1,0:T(8,128)(2,1)S(1)}, u32[]{:S(2)}, u32[]{:S(2)}) collective-permute-start(bf16[1,96,768]{2,1,0:T(8,128)(2,1)S(1)} %fusion.18), channel_id=1, source_target_pairs={{0,2},{1,3},{2,0},{3,1},{4,6},{5,7},{6,4},{7,5},{8,10},{9,11},{10,... | collective-permute-start | bytes 442376 | tf_op jit(solution)/shard_map/ppermute | solution.py:535
  263.5 15.1 %all-to-all-start.5 = ((bf16[4,128,768]{2,1,0:T(8,128)(2,1)}), bf16[4,128,768]{2,1,0:T(8,128)(2,1)S(1)}, u32[]{:S(2)}, u32[]{:S(2)}) async-start(bf16[4,128,768]{2,1,0:T(8,128)(2,1)} %pad_maximum_fusion.1), calls=%async_computation.5 | async-start | bytes 1572864 | tf_op jit(solution)/shard_map/all_to_all | solution.py:524
  (59 other events, 364.4 us)
Sparse Core Ops, SparseCore 0:
  10.8 106.9 all-gather.1

commit v3 on v2

--- a/solution.py
+++ b/solution.py
@@ -223,8 +223,7 @@
     cot_ref,
     vec_ref,
     eb_ref,
-    comb_own_ref,
-    comb_far_ref,
+    comb_ref,
     expd_own_ref,
     expd_far_ref,
     redu_own_ref,
@@ -265,9 +264,10 @@
     feats, lanes = wide // 2, msg_ref.shape[1]
     per = wide // lanes
 
-    def comb(ref, b):
-        rows = ref.shape[0] // cols2
-        return ref[b * rows : (b + 1) * rows].reshape(width, -1)[:, :step]
+    def comb(far, b):
+        rows = comb_ref.shape[0] // (2 * cols2)
+        block = 2 * b + (1 - core if far else core)
+        return comb_ref[pl.ds(block * rows, rows)].reshape(width, -1)[:, :step]
 
     @pl.when((phase == 0) & (c == 0))
     def _():
@@ -282,8 +282,8 @@
         def attend(even_ref, odd_ref):
             acc_ref[...] = beside(*[nn(at, comb(ref, b)) for b in range(cols2) for ref in (even_ref, odd_ref)])
 
-        pl.when(core == 0)(lambda: attend(comb_own_ref, comb_far_ref))
-        pl.when(core == 1)(lambda: attend(comb_far_ref, comb_own_ref))
+        pl.when(core == 0)(lambda: attend(False, True))
+        pl.when(core == 1)(lambda: attend(True, False))
         vhat, r = norm_parts(x_ref[...].astype(F32) + (acc_ref[...] + vec_ref[0:1]))
         vhat_ref[...] = vhat
         r_ref[...] = r
@@ -352,7 +352,7 @@
         pl.when(core == 1)(lambda: share(bg_away_ref, bg_here_ref))
         da = jnp.zeros(acc_ref.shape, F32)
         for b in range(cols2):
-            da = da + nt(bg_here_ref[b], comb(comb_own_ref, b)) + nt(bg_away_ref[b], comb(comb_far_ref, b))
+            da = da + nt(bg_here_ref[b], comb(False, b)) + nt(bg_away_ref[b], comb(True, b))
         acc_ref[...] = da
         tot_ref[...] = jnp.zeros_like(tot_ref)
         back = back_ref[...]
@@ -574,8 +574,8 @@
     packed = jnp.concatenate(
         [pad_lanes(expander, n_expd), pad_lanes(reducer.T, n_expd), pad_lanes(combiner, n_comb)], axis=1
     )
-    core_groups = [[r * col_n + 2 * y + k for y in range(cols2) for r in range(row_n)] for k in range(2)]
-    later = lax.all_gather(packed, mesh_axes, axis=0, tiled=True, axis_index_groups=core_groups)
+    later = lax.all_gather(packed, ("col", "row"), axis=0, tiled=True).reshape(col_n * row_n, i_rows, -1)
+
     arrived = to_seq(jnp.concatenate([inputs, cotangent], axis=1))
     x, cot = (a.reshape(tokens, width) for a in (arrived[:, :tok], arrived[:, tok:]))
     x_far = flip(x, *core_bit)
@@ -636,11 +636,8 @@
     )
     parts = reduce_part(seq_a2a(msg))
     state = seq_a2a(parts)
-    later = gate(later, parts)
-    later_far = flip(later, *core_bit).reshape(cols2 * row_n, i_rows, -1)
-    later = later.reshape(cols2 * row_n, i_rows, -1)
     def fixed(shape):
-        return pl.BlockSpec(shape, lambda p, c: (0,) * len(shape))
+        return pl.BlockSpec(shape, lambda p, c, i: (0,) * len(shape))
 
     half_shape = (cols2, tokens, n_expd)
     comb_shape = (cols2, tokens, n_com)
@@ -663,10 +660,12 @@
         msg_shape,
     ]
 
-    def weight_spec(n, place):
-        return pl.BlockSpec((row_n, i_rows, n), lambda p, c: (c // 2, 0, place))
-
-    comb_spec = pl.BlockSpec((cols2 * row_n, i_rows, n_comb), lambda p, c: (0, 0, 2 * n_expd // n_comb))
+    def weight_spec(far, place):
+        return pl.BlockSpec(
+            (row_n, i_rows, n_expd), lambda p, c, i: (c // 2 * 2 + (1 - i[0] if far else i[0]), 0, place)
+        )
+
+    comb_spec = pl.BlockSpec((col_n * row_n, i_rows, n_comb), lambda p, c, i: (0, 0, 2 * n_expd // n_comb))
     (
         attended,
         layer_out,
@@ -684,42 +683,44 @@
         ebg_away,
         dq,
         msg,
-    ) = kernel(
-        "middle",
+    ) = pl.pallas_call(
         lambda *refs: middle_kernel(scale, *refs),
-        (index, fq, state, mixed, back, x, cot, vec, ebias) + (later, later_far) * 3,
-        outs,
-        grid=(2, col_n),
-        in_specs=[
-            smem,
-            fixed(fq.shape),
-            fixed(state.shape),
-            fixed(tw),
-            fixed(back.shape),
-            fixed(tw),
-            fixed(tw),
-            fixed(vec.shape),
-            pl.BlockSpec((1, 1, n_expd), lambda p, c: (c, 0, 0)),
-            comb_spec,
-            comb_spec,
-            weight_spec(n_expd, 0),
-            weight_spec(n_expd, 0),
-            weight_spec(n_expd, 1),
-            weight_spec(n_expd, 1),
-        ],
-        out_specs=[fixed(o.shape) for o in outs],
-        scratch=[
-            pltpu.VMEM(tw, F32),
-            pltpu.VMEM(tw, F32),
-            pltpu.VMEM((tokens, 1), F32),
-            pltpu.VMEM(tw, F32),
-            pltpu.VMEM((col_n, tokens, n_expd), F32),
-            pltpu.VMEM(tw, F32),
-            pltpu.VMEM(tw, F32),
-            tot_scratch,
-        ],
-        vmem=58,
-    )
+        grid_spec=pltpu.PrefetchScalarGridSpec(
+            num_scalar_prefetch=1,
+            grid=(2, col_n),
+            in_specs=[
+                fixed(fq.shape),
+                fixed(state.shape),
+                fixed(tw),
+                fixed(back.shape),
+                fixed(tw),
+                fixed(tw),
+                fixed(vec.shape),
+                pl.BlockSpec((1, 1, n_expd), lambda p, c, i: (c, 0, 0)),
+                comb_spec,
+                weight_spec(False, 0),
+                weight_spec(True, 0),
+                weight_spec(False, 1),
+                weight_spec(True, 1),
+            ],
+            out_specs=[fixed(o.shape) for o in outs],
+            scratch_shapes=[
+                pltpu.VMEM(tw, F32),
+                pltpu.VMEM(tw, F32),
+                pltpu.VMEM((tokens, 1), F32),
+                pltpu.VMEM(tw, F32),
+                pltpu.VMEM((col_n, tokens, n_expd), F32),
+                pltpu.VMEM(tw, F32),
+                pltpu.VMEM(tw, F32),
+                tot_scratch,
+            ],
+        ),
+        out_shape=outs,
+        compiler_params=pltpu.CompilerParams(
+            dimension_semantics=("arbitrary", "arbitrary"), vmem_limit_bytes=58 * MIB
+        ),
+        name="middle",
+    )(index, fq, state, mixed, back, x, cot, vec, ebias, later, later, later, later, later)
 
     arrived = seq_a2a(msg)
 

time: 288 us -> 279 us (0.969)
  waiting for transfers between devices: 79.9 us -> 70.1 us
    pallas_call x1, Pallas kernels: 0.01 us -> 24.6 us  [on_device(): pl.pallas_call(lambda *refs: middle_kernel(scale, *refs), grid_spec=pltpu...]
    pallas_call x10 -> x9, Pallas kernels: 60.9 us -> 37 us  [kernel(): pl.pallas_call(body, grid=grid, in_specs=in_specs or [smem if a.dtype ==...]
    all_gather x1, waiting for transfers between devices: 8.69 us -> 0.01 us  [on_device(): lax.all_gather(packed, ('col', 'row'), axis=0, tiled=True)]
    ppermute x41 -> x40, waiting for transfers between devices: 62.6 us -> 62 us  [flip(): lax.ppermute(values, mesh_axes, [(d, d ^ mask) for d in range(row_n * col...]
    ppermute x41 -> x40, starting transfers between devices: 40.1 us -> 40.7 us  [flip(): lax.ppermute(values, mesh_axes, [(d, d ^ mask) for d in range(row_n * col...]
  transfers between devices with their start and end apart: 47 -> 46, of which waited for: 19 -> 18; matrix products, arithmetic and copies ran while one was open for 11% -> 11% of each run, Pallas kernels for 11% -> 11%
where the time goes in v3:
time: 279 us; the launch traced here: 277 us
  waiting for transfers between devices  70.1 us (25%)
  Pallas kernels  61.6 us (22%)
  starting transfers between devices  59.8 us (21%)
  blocking collectives  29.3 us (11%)
  local copies, waits for them, and re-layouts  21 us (8%)
  other arithmetic  20.9 us (7%)
  between operations  14.7 us (5%)
    ppermute x40, waiting for transfers between devices, flip(): lax.ppermute(values, mesh_axes, [(d, d ^ mask) for d in range(row_n * col...  62 us
    ppermute x40, starting transfers between devices, flip(): lax.ppermute(values, mesh_axes, [(d, d ^ mask) for d in range(row_n * col...  40.7 us
    pallas_call x9, Pallas kernels, kernel(): pl.pallas_call(body, grid=grid, in_specs=in_specs or [smem if a.dtype ==...  37 us
    all_to_all x1, blocking collectives, seq_a2a(): lax.all_to_all(rows, mesh_axes, split_axis=0, concat_axis=0, tiled=True,...  29.3 us
    pallas_call x1, Pallas kernels, on_device(): pl.pallas_call(lambda *refs: middle_kernel(scale, *refs), grid_spec=pltpu...  24.6 us
    all_to_all x3, starting transfers between devices, seq_a2a(): lax.all_to_all(rows, mesh_axes, split_axis=0, concat_axis=0, tiled=True,...  12.1 us
    unnamed x75, local copies, waits for them, and re-layouts  10.5 us
    convert_element_type x14, other arithmetic, rounded(): return lax.reduce_precision(a, 8, 7).astype(BF)  7.66 us
  transfers between devices with their start and end apart: 46, of which 18 were waited for; matrix products, arithmetic and copies ran while one was open for 11% of the time, Pallas kernels for 11%

profile of v3, /device:TPU:0, one launch (start us, length us, event | category | flops | bytes accessed | tf_op | source)
XLA Modules:
  0.0 277.4 jit_solution(8379666121717703249)
XLA Ops:
  9.1 4.1 %collective-permute-start.1 = (bf16[96,576]{1,0:T(8,128)(2,1)}, bf16[96,576]{1,0:T(8,128)(2,1)S(1)}, u32[]{:S(2)}, u32[]{:S(2)}) collective-permute-start(bf16[96,576]{1,0:T(8,128)(2,1)} %param.18), channel_id=1, source_target_pairs={{0,16},{1,17},{2,18},{3,19},{4,20},{5,21},{6,22},{7,23},{8,24},{9,... | collective-permute-start | bytes 331784 | tf_op jit(solution)/shard_map/ppermute | solution.py:535
  13.2 6.2 %collective-permute-done.1 = bf16[96,576]{1,0:T(8,128)(2,1)S(1)} collective-permute-done((bf16[96,576]{1,0:T(8,128)(2,1)}, bf16[96,576]{1,0:T(8,128)(2,1)S(1)}, u32[]{:S(2)}, u32[]{:S(2)}) %collective-permute-start.1) | collective-permute-done | bytes 110624 | tf_op jit(solution)/shard_map/ppermute | solution.py:535
  21.3 3.5 %all-to-all-start = ((bf16[4,128,768]{2,1,0:T(8,128)(2,1)}), bf16[4,128,768]{2,1,0:T(8,128)(2,1)S(1)}, u32[]{:S(2)}, u32[]{:S(2)}) async-start(bf16[4,128,768]{2,1,0:T(8,128)(2,1)} %pad_maximum_fusion), calls=%async_computation | async-start | bytes 1572864 | tf_op jit(solution)/shard_map/all_to_all | solution.py:524
  24.9 4.2 %collective-permute-done.2 = bf16[2,96,576]{2,1,0:T(8,128)(2,1)S(1)} collective-permute-done((bf16[2,96,576]{2,1,0:T(8,128)(2,1)S(1)}, bf16[2,96,576]{2,1,0:T(8,128)(2,1)S(1)}, u32[]{:S(2)}, u32[]{:S(2)}) %collective-permute-start.2) | collective-permute-done | bytes 221216 | tf_op jit(solution)/shard_map/ppermute | solution.py:535
  33.5 7.2 %collective-permute-done.7 = f32[576]{0:T(1024)S(1)} collective-permute-done((f32[576]{0:T(1024)S(1)}, f32[576]{0:T(1024)S(1)}, u32[]{:S(2)}, u32[]{:S(2)}) %collective-permute-start.7) | collective-permute-done | bytes 2336 | tf_op jit(solution)/shard_map/ppermute | solution.py:535
  46.0 16.2 %collective-permute-done.6 = bf16[2,2,2,96,192]{4,3,2,1,0:T(8,128)(2,1)S(1)} collective-permute-done((bf16[2,2,2,96,192]{4,3,2,1,0:T(8,128)(2,1)}, bf16[2,2,2,96,192]{4,3,2,1,0:T(8,128)(2,1)S(1)}, u32[]{:S(2)}, u32[]{:S(2)}) %collective-permute-start.6) | collective-permute-done | bytes 294944 | tf_op jit(solution)/shard_map/ppermute | solution.py:535
  66.5 3.9 %project.1 = (bf16[2,256,640]{2,1,0:T(8,128)(2,1)}, bf16[2,256,640]{2,1,0:T(8,128)(2,1)}) custom-call(bf16[256,768]{1,0:T(8,128)(2,1)} %bitcast.143, bf16[256,768]{1,0:T(8,128)(2,1)} %copy-done.4, bf16[2,768,384]{2,1,0:T(8,128)(2,1)} %maximum_select_fusion.pa_ref, bf16[2,768,192]{2,1,0:T(8,128)(2,1)} %bitcast.140, f32[2,1,640]{2,1,0:T(1,128)} %pad.16.bias_ref), custom_call_target="tpu_custom_call" | custom-call | tf_op jit(solution)/shard_map/project/pallas_call | solution.py:500
  73.7 6.2 %features.1 = (bf16[256,2304]{1,0:T(8,128)(2,1)}, bf16[6,256,512]{2,1,0:T(8,128)(2,1)}, bf16[6,256,512]{2,1,0:T(8,128)(2,1)}, bf16[1664,128]{1,0:T(8,128)(2,1)}) custom-call(s32[5]{0:T(128)} %stack.188.refs_0_.idx_ref, bf16[2,256,640]{2,1,0:T(8,128)(2,1)} %get-tuple-element.93.refs_1_, bf16[2,256,640]{2,1,0:T(8,128)(2,1)} %copy-done.12, ...), custom_call_target="tpu_custom_call" | custom-call | tf_op jit(solution)/shard_map/features/pallas_call | solution.py:500
  79.8 29.3 %all_to_all.48 = bf16[8,208,128]{2,1,0:T(8,128)(2,1)S(1)} all-to-all(bf16[8,208,128]{2,1,0:T(8,128)(2,1)} %bitcast.173), channel_id=1, replica_groups={{0,4,8,12,16,20,24,28},{1,5,9,13,17,21,25,29},{2,6,10,14,18,22,26,30},{..., dimensions={0} | all-to-all | bytes 851968 | tf_op jit(solution)/shard_map/all_to_all | solution.py:529
  110.1 3.7 %all-to-all-start.2 = ((bf16[8,208,128]{2,1,0:T(8,128)(2,1)}), bf16[8,208,128]{2,1,0:T(8,128)(2,1)S(1)}, u32[]{:S(2)}, u32[]{:S(2)}) async-start(bf16[8,208,128]{2,1,0:T(8,128)(2,1)} %tile.10), calls=%async_computation.2 | async-start | bytes 851968 | tf_op jit(solution)/shard_map/all_to_all | solution.py:529
  119.4 7.0 %all-to-all-done.2 = bf16[8,208,128]{2,1,0:T(8,128)(2,1)S(1)} async-done(((bf16[8,208,128]{2,1,0:T(8,128)(2,1)}), bf16[8,208,128]{2,1,0:T(8,128)(2,1)S(1)}, u32[]{:S(2)}, u32[]{:S(2)}) %all-to-all-start.2) | async-done | bytes 426016 | tf_op jit(solution)/shard_map/all_to_all | solution.py:529
  127.1 24.6 %middle.1 = (bf16[256,768]{1,0:T(8,128)(2,1)}, bf16[256,768]{1,0:T(8,128)(2,1)}, bf16[256,768]{1,0:T(8,128)(2,1)}, bf16[2,256,768]{2,1,0:T(8,128)(2,1)}, bf16[2,...) custom-call(s32[5]{0:T(128)} %stack.188.refs_0_.idx_ref, ...), custom_call_target="tpu_custom_call" | custom-call | tf_op jit(solution)/shard_map/middle/pallas_call | solution.py:686
  151.7 3.7 %all-to-all-start.3 = ((bf16[8,208,128]{2,1,0:T(8,128)(2,1)}), bf16[8,208,128]{2,1,0:T(8,128)(2,1)S(1)}, u32[]{:S(2)}, u32[]{:S(2)}) async-start(bf16[8,208,128]{2,1,0:T(8,128)(2,1)} %bitcast.172), calls=%async_computation.3 | async-start | bytes 851968 | tf_op jit(solution)/shard_map/all_to_all | solution.py:529
  161.1 4.2 %expander_grad.1 = (bf16[2,4,96,768]{3,2,1,0:T(8,128)(2,1)}, bf16[2,4,96,768]{3,2,1,0:T(8,128)(2,1)}) custom-call(s32[5]{0:T(128)} %stack.188.refs_0_.idx_ref, bf16[256,768]{1,0:T(8,128)(2,1)} %get-tuple-element.117.refs_1_, bf16[256,768]{1,0:T(8,128)(2,1)} %copy-done.17, bf16[2,256,768]{2,1,0:T(8,128)(2,1)} %get-tuple-element.118.refs_3_, ...), custom_call_target="tpu_custom_call" | custom-call | tf_op jit(solution)/shard_map/expander_grad/pallas_call | solution.py:500
  168.2 4.1 %reducer_grad.1 = (bf16[1,768,768]{2,1,0:T(8,128)(2,1)}, bf16[1,768,768]{2,1,0:T(8,128)(2,1)}) custom-call(s32[5]{0:T(128)} %stack.188.refs_0_.idx_ref, bf16[256,768]{1,0:T(8,128)(2,1)} %get-tuple-element.113.lh, bf16[256,768]{1,0:T(8,128)(2,1)} %copy-done.16, bf16[2,256,768]{2,1,0:T(8,128)(2,1)} %get-tuple-element.114.rh, bf16[2,256,768]{2,1,0:T(8,128)(2,1)} %copy-done.8), custom_call_target="tpu_custom_call" | custom-call | tf_op jit(solution)/shard_map/reducer_grad/pallas_call | solution.py:500
  174.5 4.6 %all-to-all-start.4 = ((bf16[8,208,128]{2,1,0:T(8,128)(2,1)}), bf16[8,208,128]{2,1,0:T(8,128)(2,1)S(1)}, u32[]{:S(2)}, u32[]{:S(2)}) async-start(bf16[8,208,128]{2,1,0:T(8,128)(2,1)} %tile.11), calls=%async_computation.4 | async-start | bytes 851968 | tf_op jit(solution)/shard_map/all_to_all | solution.py:529
  186.5 10.8 %collective-permute-done.20 = bf16[8,96,256]{2,1,0:T(8,128)(2,1)S(1)} collective-permute-done((bf16[8,96,256]{2,1,0:T(8,128)(2,1)}, bf16[8,96,256]{2,1,0:T(8,128)(2,1)S(1)}, u32[]{:S(2)}, u32[]{:S(2)}) %collective-permute-start.20) | collective-permute-done | bytes 393248 | tf_op jit(solution)/shard_map/ppermute | solution.py:535
  200.3 3.3 %reduce-precision_convert_fusion = (bf16[4,1,96,768]{3,2,1,0:T(8,128)(2,1)S(1)}, bf16[4,96,768]{2,1,0:T(8,128)(2,1)}, bf16[4,96,768]{2,1,0:T(8,128)(2,1)}, bf16[4,1,96,768]{3,2,1,0:T(8,128)(2,1)S(1)}) fusion(bf16[4,2,96,768]{3,2,1,0:T(8,128)(2,1)} %bitcast.155, s32[]{:T(128)S(6)} %select_n.369, bf16[4,2,96,768]{3,2,1,0:T(8,128)(2,1)S(1)} %bitcast.154, ...), kind=kLoop, calls=%fused_computation.1 | loop fusion | flops 5898240 | bytes 7077904 | tf_op jit(solution)/shard_map/convert_element_type | solution.py:728
  204.4 5.1 %key_back.1 = (bf16[2,256,640]{2,1,0:T(8,128)(2,1)}, bf16[2,256,640]{2,1,0:T(8,128)(2,1)}) custom-call(s32[5]{0:T(128)} %stack.188.refs_0_.idx_ref, bf16[6,256,512]{2,1,0:T(8,128)(2,1)} %get-tuple-element.99.refs_1_, bf16[1664,128]{1,0:T(8,128)(2,1)} %bitcast.151, bf16[256,2304]{1,0:T(8,128)(2,1)} %get-tuple-element.97.refs_3_, ...), custom_call_target="tpu_custom_call" | custom-call | tf_op jit(solution)/shard_map/key_back/pallas_call | solution.py:500
  212.7 4.5 %projector_grad.1 = (bf16[1,768,384]{2,1,0:T(8,128)(2,1)}, bf16[1,768,384]{2,1,0:T(8,128)(2,1)}, bf16[2,4,96,256]{3,2,1,0:T(8,128)(2,1)}, bf16[2,4,96,256]{3,2,1,0:T(8,128)(2,1)}) custom-call(s32[5]{0:T(128)} %stack.188.refs_0_.idx_ref, bf16[256,768]{1,0:T(8,128)(2,1)} %bitcast.145, bf16[256,768]{1,0:T(8,128)(2,1)} %copy-done.4, ...), custom_call_target="tpu_custom_call" | custom-call | tf_op jit(solution)/shard_map/projector_grad/pallas_call | solution.py:500
  222.1 7.5 %collective-permute-done.26 = bf16[4,96,768]{2,1,0:T(8,128)(2,1)S(1)} collective-permute-done((bf16[4,96,768]{2,1,0:T(8,128)(2,1)}, bf16[4,96,768]{2,1,0:T(8,128)(2,1)S(1)}, u32[]{:S(2)}, u32[]{:S(2)}) %collective-permute-start.26) | collective-permute-done | bytes 589856 | tf_op jit(solution)/shard_map/ppermute | solution.py:535
  239.0 4.5 %project_back.1 = (f32[256,768]{1,0:T(8,128)}, bf16[256,768]{1,0:T(8,128)(2,1)}) custom-call(bf16[2,256,640]{2,1,0:T(8,128)(2,1)} %get-tuple-element.148.refs_3_.gh_ref, bf16[2,256,640]{2,1,0:T(8,128)(2,1)} %copy-done.1, bf16[2,768,384]{2,1,0:T(8,128)(2,1)} %maximum_select_fusion.pa_ref, bf16[2,768,192]{2,1,0:T(8,128)(2,1)} %bitcast.141, ...), custom_call_target="tpu_custom_call" | custom-call | tf_op jit(solution)/shard_map/project_back/pallas_call | solution.py:500
  243.4 3.4 %collective-permute-done.32 = bf16[2,96,768]{2,1,0:T(8,128)(2,1)S(1)} collective-permute-done((bf16[2,96,768]{2,1,0:T(8,128)(2,1)S(1)}, bf16[2,96,768]{2,1,0:T(8,128)(2,1)S(1)}, u32[]{:S(2)}, u32[]{:S(2)}) %collective-permute-start.32) | collective-permute-done | bytes 294944 | tf_op jit(solution)/shard_map/ppermute | solution.py:535
  254.3 3.5 %all-to-all-start.5 = ((bf16[4,128,768]{2,1,0:T(8,128)(2,1)}), bf16[4,128,768]{2,1,0:T(8,128)(2,1)S(1)}, u32[]{:S(2)}, u32[]{:S(2)}) async-start(bf16[4,128,768]{2,1,0:T(8,128)(2,1)} %pad_maximum_fusion.1), calls=%async_computation.5 | async-start | bytes 1572864 | tf_op jit(solution)/shard_map/all_to_all | solution.py:524
  (237 shorter events, 87.4 us)
Async XLA Ops:
  7.2 119.1 %all-gather.2.cloned.1.call-start = ((), (), s32[]{:S(2)}) async-start(), calls=%async_computation.6 | async-start | bytes 11354112 | tf_op jit(solution)/shard_map/all_gather | solution.py:577
  21.3 23.1 %all-to-all-start = ((bf16[4,128,768]{2,1,0:T(8,128)(2,1)}), bf16[4,128,768]{2,1,0:T(8,128)(2,1)S(1)}, u32[]{:S(2)}, u32[]{:S(2)}) async-start(bf16[4,128,768]{2,1,0:T(8,128)(2,1)} %pad_maximum_fusion), calls=%async_computation | async-start | bytes 1572864 | tf_op jit(solution)/shard_map/all_to_all | solution.py:524
  29.4 14.4 %collective-permute-start.3 = (bf16[2,2,96,384]{3,2,1,0:T(8,128)(2,1)S(1)}, bf16[2,2,96,384]{3,2,1,0:T(8,128)(2,1)S(1)}, u32[]{:S(2)}, u32[]{:S(2)}) collective-permute-start(bf16[2,2,96,384]{3,2,1,0:T(8,128)(2,1)S(1)} %get-tuple-element.197), channel_id=1, source_target_pairs={{0,4},{1,5},{2,6},{3,7},{4,0},{5,1},{6,2},{7,3},{8,12},{9,13},{10,... | collective-permute-start | bytes 884744 | tf_op jit(solution)/shard_map/ppermute | solution.py:535
  42.2 19.9 %collective-permute-start.6 = (bf16[2,2,2,96,192]{4,3,2,1,0:T(8,128)(2,1)}, bf16[2,2,2,96,192]{4,3,2,1,0:T(8,128)(2,1)S(1)}, u32[]{:S(2)}, u32[]{:S(2)}) collective-permute-start(bf16[2,2,2,96,192]{4,3,2,1,0:T(8,128)(2,1)} %maximum_select_fusion.6), channel_id=1, source_target_pairs={{0,4},{1,5},{2,6},{3,7},{4,0},{5,1},{6,2},{7,3},{8,12},{9,13},{10,... | collective-permute-start | bytes 884744 | tf_op jit(solution)/shard_map/ppermute | solution.py:535
  43.8 19.5 %collective-permute-start.4 = (bf16[2,2,2,96,384]{4,3,1,0,2:T(8,128)(2,1)S(1)}, bf16[2,2,2,96,384]{4,3,1,0,2:T(8,128)(2,1)}, u32[]{:S(2)}, u32[]{:S(2)}) collective-permute-start(bf16[2,2,2,96,384]{4,3,1,0,2:T(8,128)(2,1)S(1)} %maximum_select_fusion.3), channel_id=1, source_target_pairs={{0,2},{1,3},{2,0},{3,1},{4,6},{5,7},{6,4},{7,5},{8,10},{9,11},{10,... | collective-permute-start | bytes 1769480 | tf_op jit(solution)/shard_map/ppermute | solution.py:535
  45.2 20.5 %collective-permute-start = (bf16[256,768]{1,0:T(8,128)(2,1)S(1)}, bf16[256,768]{1,0:T(8,128)(2,1)S(1)}, u32[]{:S(2)}, u32[]{:S(2)}) collective-permute-start(bf16[256,768]{1,0:T(8,128)(2,1)S(1)} %bitcast.142), channel_id=1, source_target_pairs={{0,1},{1,0},{2,3},{3,2},{4,5},{5,4},{6,7},{7,6},{8,9},{9,8},{10,11... | collective-permute-start | bytes 1179656 | tf_op jit(solution)/shard_map/ppermute | solution.py:535
  110.1 16.3 %all-to-all-start.2 = ((bf16[8,208,128]{2,1,0:T(8,128)(2,1)}), bf16[8,208,128]{2,1,0:T(8,128)(2,1)S(1)}, u32[]{:S(2)}, u32[]{:S(2)}) async-start(bf16[8,208,128]{2,1,0:T(8,128)(2,1)} %tile.10), calls=%async_computation.2 | async-start | bytes 851968 | tf_op jit(solution)/shard_map/all_to_all | solution.py:529
  151.7 22.0 %all-to-all-start.3 = ((bf16[8,208,128]{2,1,0:T(8,128)(2,1)}), bf16[8,208,128]{2,1,0:T(8,128)(2,1)S(1)}, u32[]{:S(2)}, u32[]{:S(2)}) async-start(bf16[8,208,128]{2,1,0:T(8,128)(2,1)} %bitcast.172), calls=%async_computation.3 | async-start | bytes 851968 | tf_op jit(solution)/shard_map/all_to_all | solution.py:529
  157.9 21.2 %collective-permute-start.19 = (f32[2,5376]{1,0:T(2,128)S(1)}, f32[2,5376]{1,0:T(2,128)S(1)}, u32[]{:S(2)}, u32[]{:S(2)}) collective-permute-start(f32[2,5376]{1,0:T(2,128)S(1)} %pad_maximum_fusion.3), channel_id=1, source_target_pairs={{0,1},{1,0},{2,3},{3,2},{4,5},{5,4},{6,7},{7,6},{8,9},{9,8},{10,11... | collective-permute-start | bytes 129032 | tf_op jit(solution)/shard_map/ppermute | solution.py:535
  159.4 20.7 %collective-permute-start.17 = (bf16[256,768]{1,0:T(8,128)(2,1)}, bf16[256,768]{1,0:T(8,128)(2,1)S(1)}, u32[]{:S(2)}, u32[]{:S(2)}) collective-permute-start(bf16[256,768]{1,0:T(8,128)(2,1)} %get-tuple-element.126.refs_1_), channel_id=1, source_target_pairs={{0,1},{1,0},{2,3},{3,2},{4,5},{5,4},{6,7},{7,6},{8,9},{9,8},{10,11... | collective-permute-start | bytes 1179656 | tf_op jit(solution)/shard_map/ppermute | solution.py:535
  160.2 19.8 %collective-permute-start.18 = (bf16[2,256,192]{2,1,0:T(8,128)(2,1)}, bf16[2,256,192]{2,1,0:T(8,128)(2,1)S(1)}, u32[]{:S(2)}, u32[]{:S(2)}) collective-permute-start(bf16[2,256,192]{2,1,0:T(8,128)(2,1)} %get-tuple-element.128), channel_id=1, source_target_pairs={{0,1},{1,0},{2,3},{3,2},{4,5},{5,4},{6,7},{7,6},{8,9},{9,8},{10,11... | collective-permute-start | bytes 589832 | tf_op jit(solution)/shard_map/ppermute | solution.py:535
  165.3 34.0 %collective-permute-start.15 = (bf16[8,96,768]{2,1,0:T(8,128)(2,1)}, bf16[8,96,768]{2,1,0:T(8,128)(2,1)S(1)}, u32[]{:S(2)}, u32[]{:S(2)}) collective-permute-start(bf16[8,96,768]{2,1,0:T(8,128)(2,1)} %bitcast.195), channel_id=1, source_target_pairs={{0,4},{1,5},{2,6},{3,7},{4,0},{5,1},{6,2},{7,3},{8,12},{9,13},{10,... | collective-permute-start | bytes 3538952 | tf_op jit(solution)/shard_map/ppermute | solution.py:535
  172.2 28.0 %collective-permute-start.16 = (bf16[8,96,768]{2,1,0:T(8,128)(2,1)}, bf16[8,96,768]{2,1,0:T(8,128)(2,1)}, u32[]{:S(2)}, u32[]{:S(2)}) collective-permute-start(bf16[8,96,768]{2,1,0:T(8,128)(2,1)} %bitcast.196), channel_id=1, source_target_pairs={{0,2},{1,3},{2,0},{3,1},{4,6},{5,7},{6,4},{7,5},{8,10},{9,11},{10,... | collective-permute-start | bytes 3538952 | tf_op jit(solution)/shard_map/ppermute | solution.py:535
  174.5 29.1 %all-to-all-start.4 = ((bf16[8,208,128]{2,1,0:T(8,128)(2,1)}), bf16[8,208,128]{2,1,0:T(8,128)(2,1)S(1)}, u32[]{:S(2)}, u32[]{:S(2)}) async-start(bf16[8,208,128]{2,1,0:T(8,128)(2,1)} %tile.11), calls=%async_computation.4 | async-start | bytes 851968 | tf_op jit(solution)/shard_map/all_to_all | solution.py:529
  209.5 20.1 %collective-permute-start.26 = (bf16[4,96,768]{2,1,0:T(8,128)(2,1)}, bf16[4,96,768]{2,1,0:T(8,128)(2,1)S(1)}, u32[]{:S(2)}, u32[]{:S(2)}) collective-permute-start(bf16[4,96,768]{2,1,0:T(8,128)(2,1)} %get-tuple-element.175), channel_id=1, source_target_pairs={{0,8},{1,9},{2,10},{3,11},{4,12},{5,13},{6,14},{7,15},{8,0},{9,1},... | collective-permute-start | bytes 1769480 | tf_op jit(solution)/shard_map/ppermute | solution.py:535
  210.9 20.8 %collective-permute-start.25 = (bf16[4,96,768]{2,1,0:T(8,128)(2,1)}, bf16[4,96,768]{2,1,0:T(8,128)(2,1)S(1)}, u32[]{:S(2)}, u32[]{:S(2)}) collective-permute-start(bf16[4,96,768]{2,1,0:T(8,128)(2,1)} %get-tuple-element.206), channel_id=1, source_target_pairs={{0,4},{1,5},{2,6},{3,7},{4,0},{5,1},{6,2},{7,3},{8,12},{9,13},{10,... | collective-permute-start | bytes 1769480 | tf_op jit(solution)/shard_map/ppermute | solution.py:535
  217.3 17.1 %collective-permute-start.24 = (bf16[8,96,384]{2,1,0:T(8,128)(2,1)}, bf16[8,96,384]{2,1,0:T(8,128)(2,1)S(1)}, u32[]{:S(2)}, u32[]{:S(2)}) collective-permute-start(bf16[8,96,384]{2,1,0:T(8,128)(2,1)} %bitcast.197), channel_id=1, source_target_pairs={{0,2},{1,3},{2,0},{3,1},{4,6},{5,7},{6,4},{7,5},{8,10},{9,11},{10,... | collective-permute-start | bytes 1769480 | tf_op jit(solution)/shard_map/ppermute | solution.py:535
  218.7 16.6 %collective-permute-start.23 = (bf16[8,96,256]{2,1,0:T(8,128)(2,1)}, bf16[8,96,256]{2,1,0:T(8,128)(2,1)S(1)}, u32[]{:S(2)}, u32[]{:S(2)}) collective-permute-start(bf16[8,96,256]{2,1,0:T(8,128)(2,1)} %bitcast.198), channel_id=1, source_target_pairs={{0,4},{1,5},{2,6},{3,7},{4,0},{5,1},{6,2},{7,3},{8,12},{9,13},{10,... | collective-permute-start | bytes 1179656 | tf_op jit(solution)/shard_map/ppermute | solution.py:535
  219.8 17.8 %collective-permute-start.22 = (bf16[4,96,256]{2,1,0:T(8,128)(2,1)}, bf16[4,96,256]{2,1,0:T(8,128)(2,1)S(1)}, u32[]{:S(2)}, u32[]{:S(2)}) collective-permute-start(bf16[4,96,256]{2,1,0:T(8,128)(2,1)} %bitcast.186), channel_id=1, source_target_pairs={{0,16},{1,17},{2,18},{3,19},{4,20},{5,21},{6,22},{7,23},{8,24},{9,... | collective-permute-start | bytes 589832 | tf_op jit(solution)/shard_map/ppermute | solution.py:535
  231.6 15.2 %collective-permute-start.32 = (bf16[2,96,768]{2,1,0:T(8,128)(2,1)S(1)}, bf16[2,96,768]{2,1,0:T(8,128)(2,1)S(1)}, u32[]{:S(2)}, u32[]{:S(2)}) collective-permute-start(bf16[2,96,768]{2,1,0:T(8,128)(2,1)S(1)} %get-tuple-element.181), channel_id=1, source_target_pairs={{0,16},{1,17},{2,18},{3,19},{4,20},{5,21},{6,22},{7,23},{8,24},{9,... | collective-permute-start | bytes 884744 | tf_op jit(solution)/shard_map/ppermute | solution.py:535
  231.9 15.4 %collective-permute-start.31 = (bf16[2,96,768]{2,1,0:T(8,128)(2,1)S(1)}, bf16[2,96,768]{2,1,0:T(8,128)(2,1)S(1)}, u32[]{:S(2)}, u32[]{:S(2)}) collective-permute-start(bf16[2,96,768]{2,1,0:T(8,128)(2,1)S(1)} %get-tuple-element.179), channel_id=1, source_target_pairs={{0,8},{1,9},{2,10},{3,11},{4,12},{5,13},{6,14},{7,15},{8,0},{9,1},... | collective-permute-start | bytes 884744 | tf_op jit(solution)/shard_map/ppermute | solution.py:535
  234.5 14.9 %collective-permute-start.30 = (bf16[4,96,384]{2,1,0:T(8,128)(2,1)S(1)}, bf16[4,96,384]{2,1,0:T(8,128)(2,1)S(1)}, u32[]{:S(2)}, u32[]{:S(2)}) collective-permute-start(bf16[4,96,384]{2,1,0:T(8,128)(2,1)S(1)} %get-tuple-element.177), channel_id=1, source_target_pairs={{0,4},{1,5},{2,6},{3,7},{4,0},{5,1},{6,2},{7,3},{8,12},{9,13},{10,... | collective-permute-start | bytes 884744 | tf_op jit(solution)/shard_map/ppermute | solution.py:535
  247.2 15.5 %collective-permute-start.38 = (bf16[1,96,768]{2,1,0:T(8,128)(2,1)S(1)}, bf16[1,96,768]{2,1,0:T(8,128)(2,1)S(1)}, u32[]{:S(2)}, u32[]{:S(2)}) collective-permute-start(bf16[1,96,768]{2,1,0:T(8,128)(2,1)S(1)} %fusion.18), channel_id=1, source_target_pairs={{0,2},{1,3},{2,0},{3,1},{4,6},{5,7},{6,4},{7,5},{8,10},{9,11},{10,... | collective-permute-start | bytes 442376 | tf_op jit(solution)/shard_map/ppermute | solution.py:535
  254.3 15.1 %all-to-all-start.5 = ((bf16[4,128,768]{2,1,0:T(8,128)(2,1)}), bf16[4,128,768]{2,1,0:T(8,128)(2,1)S(1)}, u32[]{:S(2)}, u32[]{:S(2)}) async-start(bf16[4,128,768]{2,1,0:T(8,128)(2,1)} %pad_maximum_fusion.1), calls=%async_computation.5 | async-start | bytes 1572864 | tf_op jit(solution)/shard_map/all_to_all | solution.py:524
  (58 other events, 384.1 us)
Sparse Core Ops, SparseCore 0:
  11.0 108.2 all-gather.1
